TPU v7x, 32 devices: a whole 2x2x4 slice. The times are simulated.
32 devices in a mesh: batch: 4 (over x, core), seq: 8 (over z, y).
Axes of the slice: x: 2, y: 2, z: 4, core: 2. Of those that a mesh axis runs over, the one named last changes fastest.
Arguments:
- tokens: bfloat16 [8, 1024, 768], P('batch', 'seq'), may hold values from -6 to 6
- in_proj: bfloat16 [768, 3072], P(('batch', 'seq')), may hold values from -0.21875 to 0.21875
- conv_weight: bfloat16 [4, 1536], P(None, ('batch', 'seq')), may hold values from -3 to 3
- conv_bias: bfloat16 [1536], P(('batch', 'seq')), may hold values from -1.5 to 1.5
- state_proj: bfloat16 [1536, 80], P(('batch', 'seq')), may hold values from -0.15625 to 0.15625
- step_proj: bfloat16 [48, 1536], P(None, ('batch', 'seq')), may hold values from -0.875 to 0.875
- step_bias: bfloat16 [1536], P(('batch', 'seq')), may hold values from -3 to -1
- decay_log: bfloat16 [16, 1536], P(None, ('batch', 'seq'))
- skip_gain: bfloat16 [1536], P(('batch', 'seq')), may hold values from 0.5 to 1.5
- out_proj: bfloat16 [1536, 768], P(('batch', 'seq')), may hold values from -0.0390625 to 0.0390625
- norm_gain: bfloat16 [768], P(('batch', 'seq')), may hold values from 0.5 to 1.5
- moe_gain: bfloat16 [768], P(('batch', 'seq')), may hold values from 0.5 to 1.5
- router_proj: bfloat16 [768, 8], P(('batch', 'seq')), may hold values from -0.14941406 to 0.14941406
- expert_up: bfloat16 [8, 768, 3072], P('seq', None, 'batch'), may hold values from -0.21875 to 0.21875
- expert_down: bfloat16 [8, 3072, 768], P('seq', 'batch'), may hold values from -0.21875 to 0.21875
- routes: int32 [8, 1024], P('batch', 'seq'), may hold values from 0 to 7, as said below
- slot_index: int32 [8, 1024], P('batch', 'seq'), may hold values from 0 to 79, as said below
- cotangent: bfloat16 [8, 1024, 768], P('batch', 'seq'), may hold values from -6 to 6
Outputs:
- block_out: bfloat16 [8, 1024, 768], P('batch', 'seq')
- d_tokens: float32 [8, 1024, 768], P('batch', 'seq')
- d_in_proj: float32 [768, 3072], P(('batch', 'seq'))
- d_conv_weight: float32 [4, 1536], P(None, ('batch', 'seq'))
- d_conv_bias: float32 [1536], P(('batch', 'seq'))
- d_state_proj: float32 [1536, 80], P(('batch', 'seq'))
- d_step_proj: float32 [48, 1536], P(None, ('batch', 'seq'))
- d_step_bias: float32 [1536], P(('batch', 'seq'))
- d_decay_log: float32 [16, 1536], P(None, ('batch', 'seq'))
- d_skip_gain: float32 [1536], P(('batch', 'seq'))
- d_out_proj: float32 [1536, 768], P(('batch', 'seq'))
- d_norm_gain: float32 [768], P(('batch', 'seq'))
- d_moe_gain: float32 [768], P(('batch', 'seq'))
- d_router_proj: float32 [768, 8], P(('batch', 'seq'))
- d_expert_up: float32 [8, 768, 3072], P('seq', None, 'batch')
- d_expert_down: float32 [8, 3072, 768], P('seq', 'batch')
Inputs may be any that keep to these rules, and one draw needn't show every extreme that they name: `routes`: each token's expert; among the tokens of one device, one expert is named by exactly min(256, 80) of them and every other expert by fewer. `slot_index`: the number of earlier tokens with the same expert among the 256 tokens of the same device, counted over its sequences in order and positions in order within each.
All inputs are finite; a program needn't handle non-finite values.
Results may differ from a plain program's by a relative error of at most 0.018.
Values may be sent and summed in bfloat16 or wider, within the bound.
A program may use at most 192 MiB of HBM per device.

v0:
```python
from functools import partial
import math

import jax
import jax.numpy as jnp
from jax import lax
from jax.sharding import PartitionSpec as P

epsilon = 1e-05


def from_behind(block, axis, distance):
    devices = range(lax.axis_size(axis))
    route = [(i - distance, i) for i in devices if i - distance in devices]
    return lax.ppermute(block, axis, route)


def prefix(shard, axis, combine, identity):
    peers, here = (lax.axis_size(axis), lax.axis_index(axis))
    everything = jax.tree.map(
        lambda part, kind: lax.all_gather(part.astype(kind), axis),
        shard,
        (jnp.bfloat16, jnp.bfloat16),
    )
    start = jax.tree.map(
        lambda part, zero: jnp.broadcast_to(jnp.asarray(zero, part.dtype), part.shape),
        shard,
        identity,
    )

    def hop(k, before):
        reached = k < here
        new = combine(
            before, jax.tree.map(lambda part, own: part[k].astype(own.dtype), everything, shard)
        )
        return jax.tree.map(lambda a, b: jnp.where(reached, a, b), new, before)

    return lax.fori_loop(0, peers, hop, start)


def prefix_2(shard, axis, join, neutral):
    count = lax.axis_size(axis)
    place = lax.axis_index(axis)
    ahead = count - 1 - place
    gathered = jax.tree.map(
        lambda a, kind: lax.all_gather(a.astype(kind), axis),
        shard,
        jax.tree.map(lambda a: jnp.bfloat16 if a.dtype == jnp.float32 else a.dtype, shard),
    )
    state = jax.tree.map(lambda a, e: jnp.zeros_like(a) + jnp.asarray(e, a.dtype), shard, neutral)

    def one(hop, state):
        source = count - 1 - hop
        return join(
            state,
            jax.tree.map(
                lambda a, own: lax.dynamic_index_in_dim(a, source, 0, False).astype(own.dtype),
                gathered,
                shard,
            ),
        )

    return lax.fori_loop(0, ahead, one, state)


def as_sent(shard):

    def short(part):
        return part.astype(jnp.bfloat16) if part.dtype == jnp.float32 else part

    return jax.tree.map(short, shard)


def chain_combine(earlier, later):
    return (earlier[0] * later[0], later[0] * earlier[1] + later[1])


def conv_local(extended, kernel, bias_term):
    kernel_len = kernel.shape[0]
    row_count = extended.shape[1] - kernel_len + 1
    conv_total = bias_term + jnp.zeros_like(extended[:, :row_count])
    for offset in range(kernel_len):
        conv_total = conv_total + kernel[offset] * extended[:, offset : offset + row_count]
    return jax.nn.silu(conv_total)


def advance(decay_rates, running, inputs):
    now_dt, now_u, now_b, now_c = inputs
    decay_now = jnp.exp(now_dt[:, None, :] * decay_rates[None])
    running = decay_now * running + now_b[:, :, None] * (now_dt * now_u)[:, None, :]
    return (running, jnp.sum(running * now_c[:, :, None], axis=1))


def regroup_blocks(value_entries, block_length):
    seq_count, row_count, feature_count = value_entries.shape
    return jnp.swapaxes(value_entries, 0, 1).reshape(
        row_count // block_length, block_length, seq_count, feature_count
    )


def zero_scan(step_delta, activated_input, input_matrix_b, input_matrix_c, decay_rates):
    seq_count, row_count, inner_width = step_delta.shape
    block_length = math.gcd(row_count, 16)
    blocks = (
        regroup_blocks(step_delta, block_length),
        regroup_blocks(activated_input, block_length),
        regroup_blocks(input_matrix_b, block_length),
        regroup_blocks(input_matrix_c, block_length),
    )

    def through_block(running, block):
        return lax.scan(partial(advance, decay_rates), running, block)

    start_state = jnp.zeros((seq_count, decay_rates.shape[0], inner_width), jnp.float32)
    end_state, outputs = lax.scan(jax.checkpoint(through_block), start_state, blocks)
    outputs = jnp.swapaxes(outputs.reshape(row_count, seq_count, inner_width), 0, 1)
    return (outputs, end_state)


def start_terms(start_state, step_delta, input_matrix_c, decay_rates):
    reach = jnp.exp(decay_rates[None, None] * jnp.cumsum(step_delta, axis=1)[:, :, None, :])
    outputs = jnp.sum(reach * (input_matrix_c[:, :, :, None] * start_state[:, None]), axis=2)
    carried = reach[:, -1] * start_state
    return (outputs, carried)


def body(
    tokens,
    in_proj,
    conv_weight,
    conv_bias,
    state_proj,
    step_proj,
    step_bias,
    decay_log,
    skip_gain,
    out_proj,
    norm_gain,
    moe_gain,
    router_proj,
    expert_up,
    expert_down,
    routes,
    slot_index,
    cotangent,
):
    fetched = (
        lax.all_gather(in_proj, ("batch", "seq"), axis=0, tiled=True),
        lax.all_gather(conv_weight, ("batch", "seq"), axis=1, tiled=True),
        lax.all_gather(conv_bias, ("batch", "seq"), axis=0, tiled=True),
        lax.all_gather(state_proj, ("batch", "seq"), axis=0, tiled=True),
        lax.all_gather(step_proj, ("batch", "seq"), axis=1, tiled=True),
        lax.all_gather(step_bias, ("batch", "seq"), axis=0, tiled=True),
        lax.all_gather(decay_log, ("batch", "seq"), axis=1, tiled=True),
        lax.all_gather(skip_gain, ("batch", "seq"), axis=0, tiled=True),
        lax.all_gather(out_proj, ("batch", "seq"), axis=0, tiled=True),
        lax.all_gather(norm_gain, ("batch", "seq"), axis=0, tiled=True),
        lax.all_gather(moe_gain, ("batch", "seq"), axis=0, tiled=True),
        lax.all_gather(router_proj, ("batch", "seq"), axis=0, tiled=True),
    )
    experts_full = (expert_up, expert_down)
    experts_full = (
        lax.all_gather(expert_up, "batch", axis=2, tiled=True),
        lax.all_gather(expert_down, "batch", axis=1, tiled=True),
    )
    (
        in_full,
        conv_w_full,
        conv_b_full,
        state_full,
        step_full,
        step_bias_full,
        decay_full,
        skip_full,
        out_full,
        norm_full,
        moe_full,
        router_full,
    ) = fetched
    seq_count, row_count, model_width = tokens.shape
    token_count = seq_count * row_count
    inner_width = skip_full.shape[0]
    state_count = decay_full.shape[0]
    rank_count = step_full.shape[0]
    kernel_len = conv_w_full.shape[0]
    local_experts = expert_up.shape[0]
    expert_count = local_experts * lax.axis_size("seq")
    capacity = max(2, 5 * token_count // (4 * expert_count))
    resid = tokens.astype(jnp.float32)
    rms_one = lax.rsqrt(jnp.mean(resid * resid, axis=-1, keepdims=True) + epsilon)
    norm_gain_f = norm_full.astype(jnp.float32)
    normed = (resid * rms_one * norm_gain_f).astype(jnp.bfloat16)
    mixed = jnp.einsum("std,de->ste", normed, in_full, preferred_element_type=jnp.float32)
    inner_x = mixed[..., :inner_width]
    gate_z = mixed[..., inner_width:]
    tail = from_behind(
        inner_x[:, row_count - kernel_len + 1 :].astype(jnp.bfloat16), "seq", 1
    ).astype(jnp.float32)
    extended = jnp.concatenate([tail, inner_x], axis=1)
    activated_input, conv_back = jax.vjp(
        conv_local, extended, conv_w_full.astype(jnp.float32), conv_b_full.astype(jnp.float32)
    )
    u_low = activated_input.astype(jnp.bfloat16)
    projected = jnp.einsum("sti,ij->stj", u_low, state_full, preferred_element_type=jnp.float32)
    rank_low = projected[..., :rank_count].astype(jnp.bfloat16)
    input_matrix_b = projected[..., rank_count : rank_count + state_count]
    input_matrix_c = projected[..., rank_count + state_count :]
    step_pre = jnp.einsum(
        "str,ri->sti", rank_low, step_full, preferred_element_type=jnp.float32
    ) + step_bias_full.astype(jnp.float32)
    step_delta = jax.nn.softplus(step_pre)
    decay_rates = -jnp.exp(decay_full.astype(jnp.float32))
    (zero_out, zero_end), zero_back = jax.vjp(
        zero_scan, step_delta, activated_input, input_matrix_b, input_matrix_c, decay_rates
    )
    total_decay = jnp.exp(decay_rates[None] * jnp.sum(step_delta, axis=1)[:, None, :])
    prefix_pair = prefix(
        (total_decay, zero_end),
        "seq",
        chain_combine,
        (jnp.ones_like(total_decay), jnp.zeros_like(total_decay)),
    )
    (start_out, start_end), start_back = jax.vjp(
        start_terms, prefix_pair[1], step_delta, input_matrix_c, decay_rates
    )
    scan_out = zero_out + start_out
    skip_f = skip_full.astype(jnp.float32)
    gate_silu, silu_back = jax.vjp(jax.nn.silu, gate_z)
    mamba_y = scan_out + skip_f * activated_input
    gated_low = (mamba_y * gate_silu).astype(jnp.bfloat16)
    branch_out = jnp.einsum("sti,id->std", gated_low, out_full, preferred_element_type=jnp.float32)
    hidden_one = (resid + branch_out).reshape(token_count, model_width)
    rms_two = lax.rsqrt(jnp.mean(hidden_one * hidden_one, axis=-1, keepdims=True) + epsilon)
    moe_gain_f = moe_full.astype(jnp.float32)
    flat_in = (hidden_one * rms_two * moe_gain_f).astype(jnp.bfloat16)
    logits = jnp.dot(flat_in, router_full, preferred_element_type=jnp.float32)
    flat_route = routes.reshape(token_count)
    flat_slot = slot_index.reshape(token_count)
    picked = (flat_route[:, None] == jnp.arange(expert_count, dtype=jnp.int32)[None, :]).astype(
        jnp.float32
    )
    gate_prob = jax.nn.sigmoid(jnp.sum(logits * picked, axis=1))
    kept = (flat_slot < capacity).astype(jnp.float32)
    clipped = jnp.minimum(flat_slot, capacity - 1)
    send_buffer = (
        jnp.zeros((expert_count, capacity, model_width), jnp.bfloat16)
        .at[flat_route, flat_slot]
        .set(flat_in, mode="drop")
    )
    received = lax.all_to_all(send_buffer, "seq", split_axis=0, concat_axis=0, tiled=True)
    source_count = received.shape[0] // local_experts
    grouped = received.reshape(source_count, local_experts, received.shape[1], model_width)
    hidden = jnp.einsum(
        "sxcd,xdf->sxcf", grouped, experts_full[0], preferred_element_type=jnp.float32
    )
    activated = jax.nn.gelu(hidden, approximate=False).astype(jnp.bfloat16)
    results = (
        jnp.einsum("sxcf,xfd->sxcd", activated, experts_full[1], preferred_element_type=jnp.float32)
        .astype(jnp.bfloat16)
        .reshape(received.shape)
    )
    returned = lax.all_to_all(results, "seq", split_axis=0, concat_axis=0, tiled=True)
    expert_rows = returned[flat_route, clipped].astype(jnp.float32) * kept[:, None]
    combined = hidden_one + gate_prob[:, None] * expert_rows
    block_out = combined.reshape(tokens.shape).astype(jnp.bfloat16)
    grad_out = cotangent.reshape(token_count, model_width).astype(jnp.float32)
    grad_gate = jnp.sum(grad_out * expert_rows, axis=1)
    grad_logit_low = (picked * (grad_gate * gate_prob * (1.0 - gate_prob))[:, None]).astype(
        jnp.bfloat16
    )
    grad_rows_low = (grad_out * (gate_prob * kept)[:, None]).astype(jnp.bfloat16)
    grad_buffer = (
        jnp.zeros((expert_count, capacity, model_width), jnp.bfloat16)
        .at[flat_route, flat_slot]
        .set(grad_rows_low, mode="drop")
    )
    fetched = (
        lax.all_gather(in_proj, ("batch", "seq"), axis=0, tiled=True),
        lax.all_gather(conv_weight, ("batch", "seq"), axis=1, tiled=True),
        lax.all_gather(conv_bias, ("batch", "seq"), axis=0, tiled=True),
        lax.all_gather(state_proj, ("batch", "seq"), axis=0, tiled=True),
        lax.all_gather(step_proj, ("batch", "seq"), axis=1, tiled=True),
        lax.all_gather(step_bias, ("batch", "seq"), axis=0, tiled=True),
        lax.all_gather(decay_log, ("batch", "seq"), axis=1, tiled=True),
        lax.all_gather(skip_gain, ("batch", "seq"), axis=0, tiled=True),
        lax.all_gather(out_proj, ("batch", "seq"), axis=0, tiled=True),
        lax.all_gather(norm_gain, ("batch", "seq"), axis=0, tiled=True),
        lax.all_gather(moe_gain, ("batch", "seq"), axis=0, tiled=True),
        lax.all_gather(router_proj, ("batch", "seq"), axis=0, tiled=True),
    )
    (
        in_full,
        conv_w_full,
        conv_b_full,
        state_full,
        step_full,
        step_bias_full,
        decay_full,
        skip_full,
        out_full,
        norm_full,
        moe_full,
        router_full,
    ) = fetched
    received_grad = lax.all_to_all(grad_buffer, "seq", split_axis=0, concat_axis=0, tiled=True)
    source_count = received_grad.shape[0] // local_experts
    rows_in, rows_grad = (received, received_grad)
    experts_full = (
        lax.all_gather(expert_up, "batch", axis=2, tiled=True),
        lax.all_gather(expert_down, "batch", axis=1, tiled=True),
    )
    up_use, down_use = experts_full
    grouped_in = rows_in.reshape(source_count, local_experts, rows_in.shape[1], model_width)
    grouped_grad = rows_grad.reshape(source_count, local_experts, rows_grad.shape[1], model_width)
    hidden = jnp.einsum("sxcd,xdf->sxcf", grouped_in, up_use, preferred_element_type=jnp.float32)
    activated, gelu_back = jax.vjp(partial(jax.nn.gelu, approximate=False), hidden)
    grad_down = jnp.einsum(
        "sxcf,sxcd->xfd",
        activated.astype(jnp.bfloat16),
        grouped_grad,
        preferred_element_type=jnp.float32,
    )
    grad_act = jnp.einsum(
        "sxcd,xfd->sxcf", grouped_grad, down_use, preferred_element_type=jnp.float32
    )
    grad_hidden = gelu_back(grad_act)[0].astype(jnp.bfloat16)
    grad_up = jnp.einsum(
        "sxcd,sxcf->xdf", grouped_in, grad_hidden, preferred_element_type=jnp.float32
    )
    input_terms = jnp.einsum(
        "sxcf,xdf->sxcd", grad_hidden, up_use, preferred_element_type=jnp.float32
    )
    grad_inputs = input_terms.reshape(received_grad.shape).astype(jnp.bfloat16)
    expert_sums = (
        lax.psum_scatter(
            grad_up.astype(jnp.bfloat16), "batch", scatter_dimension=2, tiled=True
        ).astype(jnp.float32),
        lax.psum_scatter(
            grad_down.astype(jnp.bfloat16), "batch", scatter_dimension=1, tiled=True
        ).astype(jnp.float32),
    )
    returned_grad = lax.all_to_all(grad_inputs, "seq", split_axis=0, concat_axis=0, tiled=True)
    grad_moe_in = returned_grad[flat_route, clipped].astype(jnp.float32) * kept[:, None]
    grad_moe_in = grad_moe_in + jnp.einsum(
        "te,de->td", grad_logit_low, router_full, preferred_element_type=jnp.float32
    )
    grad_router = jnp.einsum(
        "td,te->de", flat_in, grad_logit_low, preferred_element_type=jnp.float32
    )
    scaled_two = hidden_one * rms_two
    grad_moe_gain = jnp.sum(grad_moe_in * scaled_two, axis=0)
    grad_scaled_two = grad_moe_in * moe_gain_f
    grad_hidden_one = (
        grad_out
        + rms_two * grad_scaled_two
        - hidden_one
        * (rms_two * rms_two * rms_two)
        * jnp.mean(grad_scaled_two * hidden_one, axis=1, keepdims=True)
    )
    grad_hidden_one = grad_hidden_one.reshape(tokens.shape)
    grad_branch_low = grad_hidden_one.astype(jnp.bfloat16)
    grad_out_proj = jnp.einsum(
        "sti,std->id", gated_low, grad_branch_low, preferred_element_type=jnp.float32
    )
    grad_gated = jnp.einsum(
        "std,id->sti", grad_branch_low, out_full, preferred_element_type=jnp.float32
    )
    grad_y = grad_gated * gate_silu
    grad_z = silu_back(grad_gated * mamba_y)[0]
    grad_skip = jnp.sum(grad_y * activated_input, axis=(0, 1))
    local_pull = start_back((grad_y, jnp.zeros_like(start_end)))
    back_pair = prefix_2(
        (total_decay, local_pull[0]),
        "seq",
        chain_combine,
        (jnp.ones_like(total_decay), jnp.zeros_like(total_decay)),
    )
    later_adjoint = back_pair[1]
    end_pull = start_back((jnp.zeros_like(grad_y), later_adjoint))
    zero_pull = zero_back((grad_y, later_adjoint))
    grad_dt = zero_pull[0] + local_pull[1] + end_pull[1]
    grad_u_scan = zero_pull[1]
    grad_b = zero_pull[2]
    grad_c = zero_pull[3] + local_pull[2] + end_pull[2]
    grad_decay_log = (zero_pull[4] + local_pull[3] + end_pull[3]) * decay_rates
    grad_pre = grad_dt * jax.nn.sigmoid(step_pre)
    grad_step_bias = jnp.sum(grad_pre, axis=(0, 1))
    grad_pre_low = grad_pre.astype(jnp.bfloat16)
    grad_step_proj = jnp.einsum(
        "str,sti->ri", rank_low, grad_pre_low, preferred_element_type=jnp.float32
    )
    grad_rank = jnp.einsum(
        "sti,ri->str", grad_pre_low, step_full, preferred_element_type=jnp.float32
    )
    grad_proj_low = jnp.concatenate([grad_rank, grad_b, grad_c], axis=-1).astype(jnp.bfloat16)
    grad_state_proj = jnp.einsum(
        "sti,stj->ij", u_low, grad_proj_low, preferred_element_type=jnp.float32
    )
    grad_u = (
        jnp.einsum("stj,ij->sti", grad_proj_low, state_full, preferred_element_type=jnp.float32)
        + grad_y * skip_f
        + grad_u_scan
    )
    grad_extended, grad_conv_w, grad_conv_b = conv_back(grad_u)
    from_next = from_behind(as_sent(grad_extended[:, : kernel_len - 1]), "seq", -1)
    grad_inner = (
        grad_extended[:, kernel_len - 1 :].at[:, row_count - kernel_len + 1 :].add(from_next)
    )
    grad_mixed_low = jnp.concatenate([grad_inner, grad_z], axis=-1).astype(jnp.bfloat16)
    grad_in_proj = jnp.einsum(
        "std,ste->de", normed, grad_mixed_low, preferred_element_type=jnp.float32
    )
    grad_normed = jnp.einsum(
        "ste,de->std", grad_mixed_low, in_full, preferred_element_type=jnp.float32
    )
    scaled_one = resid * rms_one
    grad_norm_gain = jnp.sum(grad_normed * scaled_one, axis=(0, 1))
    grad_scaled_one = grad_normed * norm_gain_f
    grad_tokens = (
        grad_hidden_one
        + rms_one * grad_scaled_one
        - resid
        * (rms_one * rms_one * rms_one)
        * jnp.mean(grad_scaled_one * resid, axis=-1, keepdims=True)
    )
    summed = (
        lax.psum_scatter(grad_in_proj, ("batch", "seq"), scatter_dimension=0, tiled=True),
        lax.psum_scatter(grad_conv_w, ("batch", "seq"), scatter_dimension=1, tiled=True),
        lax.psum_scatter(grad_conv_b, ("batch", "seq"), scatter_dimension=0, tiled=True),
        lax.psum_scatter(grad_state_proj, ("batch", "seq"), scatter_dimension=0, tiled=True),
        lax.psum_scatter(grad_step_proj, ("batch", "seq"), scatter_dimension=1, tiled=True),
        lax.psum_scatter(grad_step_bias, ("batch", "seq"), scatter_dimension=0, tiled=True),
        lax.psum_scatter(grad_decay_log, ("batch", "seq"), scatter_dimension=1, tiled=True),
        lax.psum_scatter(grad_skip, ("batch", "seq"), scatter_dimension=0, tiled=True),
        lax.psum_scatter(grad_out_proj, ("batch", "seq"), scatter_dimension=0, tiled=True),
        lax.psum_scatter(grad_norm_gain, ("batch", "seq"), scatter_dimension=0, tiled=True),
        lax.psum_scatter(grad_moe_gain, ("batch", "seq"), scatter_dimension=0, tiled=True),
        lax.psum_scatter(grad_router, ("batch", "seq"), scatter_dimension=0, tiled=True),
    )
    return (
        block_out,
        grad_tokens,
        summed[0],
        summed[1],
        summed[2],
        summed[3],
        summed[4],
        summed[5],
        summed[6],
        summed[7],
        summed[8],
        summed[9],
        summed[10],
        summed[11],
        expert_sums[0],
        expert_sums[1],
    )


def solution(mesh):
    in_specs = (
        P("batch", "seq", None),
        P(("batch", "seq"), None),
        P(None, ("batch", "seq")),
        P(("batch", "seq")),
        P(("batch", "seq"), None),
        P(None, ("batch", "seq")),
        P(("batch", "seq")),
        P(None, ("batch", "seq")),
        P(("batch", "seq")),
        P(("batch", "seq"), None),
        P(("batch", "seq")),
        P(("batch", "seq")),
        P(("batch", "seq"), None),
        P("seq", None, "batch"),
        P("seq", "batch", None),
        P("batch", "seq"),
        P("batch", "seq"),
        P("batch", "seq", None),
    )
    out_specs = (
        P("batch", "seq", None),
        P("batch", "seq", None),
        P(("batch", "seq"), None),
        P(None, ("batch", "seq")),
        P(("batch", "seq")),
        P(("batch", "seq"), None),
        P(None, ("batch", "seq")),
        P(("batch", "seq")),
        P(None, ("batch", "seq")),
        P(("batch", "seq")),
        P(("batch", "seq"), None),
        P(("batch", "seq")),
        P(("batch", "seq")),
        P(("batch", "seq"), None),
        P("seq", None, "batch"),
        P("seq", "batch", None),
    )
    return jax.shard_map(body, mesh=mesh, in_specs=in_specs, out_specs=out_specs, check_vma=False)
```

profile of v0, /device:TPU:0, one launch (start us, length us, event | category | flops | bytes accessed | tf_op | source)
XLA Modules:
  0.0 2255.7 jit_solution(982527725874089681)
XLA Ops:
  14.2 42.6 %all-reduce.22 = (bf16[1536]{0:T(1024)(128)(2,1)S(1)}, bf16[768]{0:T(1024)(128)(2,1)S(1)}, bf16[1536]{0:T(1024)(128)(2,1)S(1)}, bf16[1536]{0:T(1024)(128)(2,1)S(1)}, bf16[768]{0:T(1024)(128)(2,1)S(1)}) all-reduce(bf16[1536]{0:T(1024)(128)(2,1)S(1)} %dynamic-update-slice.5, ...), channel_id=1, replica_groups=mesh['batch'=4,'seq'=8] {'batch','seq'}, use_global_device_ids=true, to_apply=%add.12 | all-reduce | flops 6144 | bytes 24576
  58.6 66.1 %all-gather.1 = bf16[32,48,4]{1,2,0:T(4,128)(2,1)S(1)} all-gather(bf16[1,48,4]{1,2,0:T(4,128)(2,1)} %bitcast.573), channel_id=1, replica_groups=mesh['batch'=4,'seq'=8] {'batch','seq'}, dimensions={0}, use_global_device_ids=true | all-gather | bytes 12672 | tf_op jit(solution)/shard_map/all_gather | solution.py:149
  125.7 66.9 %all_gather.69 = bf16[1536,80]{1,0:T(8,128)(2,1)S(1)} all-gather(bf16[48,80]{1,0:T(8,128)(2,1)} %param.38), channel_id=1, replica_groups=mesh['batch'=4,'seq'=8] {'batch','seq'}, dimensions={0}, use_global_device_ids=true | all-gather | bytes 253440 | tf_op jit(solution)/shard_map/all_gather | solution.py:151
  192.7 66.8 %all-gather.2 = bf16[32,48,16]{1,2,0:T(8,128)(2,1)S(1)} all-gather(bf16[1,48,16]{1,2,0:T(8,128)(2,1)} %bitcast.571), channel_id=1, replica_groups=mesh['batch'=4,'seq'=8] {'batch','seq'}, dimensions={0}, use_global_device_ids=true | all-gather | bytes 50688 | tf_op jit(solution)/shard_map/all_gather | solution.py:154
  267.1 65.7 %all_gather.70 = bf16[48,1536]{0,1:T(8,128)(2,1)S(1)} all-gather(bf16[48,48]{0,1:T(8,128)(2,1)S(1)} %copy.140), channel_id=1, replica_groups=mesh['batch'=4,'seq'=8] {'batch','seq'}, dimensions={1}, use_global_device_ids=true | all-gather | bytes 152064 | tf_op jit(solution)/shard_map/all_gather | solution.py:152
  341.1 34.1 %all_gather.73 = bf16[8,2,16,1536]{3,2,1,0:T(8,128)(2,1)} all-gather(bf16[1,2,16,1536]{3,2,1,0:T(8,128)(2,1)S(1)} %exponential_convert_fusion), channel_id=1, replica_groups=mesh['batch'=4,'seq'=8] {'seq'}, dimensions={0}, use_global_device_ids=true | all-gather | bytes 884736 | tf_op jit(solution)/shard_map/all_gather | solution.py:21
  382.8 54.0 %while.196 = (s32[]{:T(128)}, f32[2,16,1536]{2,1,0:T(8,128)S(1)}, f32[8,16,2,1536]{3,1,0,2:T(8,128)}, f32[8,2,16,1536]{3,2,1,0:T(8,128)}, f32[8,16,2,1536]{3,2,1...) while((s32[]{:T(128)}, f32[2,16,1536]{2,1,0:T(8,128)S(1)}, ...), condition=%wide.region_5.6_spmd, body=%wide.region_1.5_spmd.sunk | while | flops 294916 | bytes 2196562 | solution.py:115
  436.9 33.8 %all-gather = bf16[16,16,1536]{2,1,0:T(8,128)(2,1)} all-gather(bf16[2,16,1536]{2,1,0:T(8,128)(2,1)S(1)} %convert_element_type.201), channel_id=2, replica_groups=mesh['batch'=4,'seq'=8] {'seq'}, dimensions={0}, use_global_device_ids=true | all-gather | bytes 884736 | tf_op jit(solution)/shard_map/all_gather | solution.py:21
  512.1 35.7 %scatter_fusion = bf16[8,40,768]{2,1,0:T(8,128)(2,1)} fusion(bf16[8,40,768]{2,1,0:T(8,128)(2,1)} %broadcast.458.clone, s32[256]{0:T(256)S(1)} %bitcast.539, bf16[256,768]{1,0:T(8,128)(2,1)} %multiply_convert_fusion.1), kind=kCustom, calls=%fused_computation.2 | custom fusion | bytes 1181696 | tf_op jit(solution)/shard_map/scatter | solution.py:248
  585.0 67.2 %all-gather.3 = bf16[32,24,8]{1,2,0:T(8,128)(2,1)S(1)} all-gather(bf16[1,24,8]{1,2,0:T(8,128)(2,1)} %bitcast.572), channel_id=1, replica_groups=mesh['batch'=4,'seq'=8] {'batch','seq'}, dimensions={0}, use_global_device_ids=true | all-gather | bytes 12672 | tf_op jit(solution)/shard_map/all_gather | solution.py:159
  754.4 46.6 %multiply_reduce_fusion.6 = (f32[16,1536]{1,0:T(8,128)}, f32[2,128,1536]{2,0,1:T(2,128)}, f32[2,128,16]{2,0,1:T(2,128)}, f32[2,16,1536]{2,1,0:T(8,128)}, f32[2,128,16]{2,0,1:T(2,128)}, /*index=5*/f32[2,128,16,1536]{3,2,0,1:T(8,128)}) fusion(f32[2,1,16,1536]{3,2,0,1:T(8,128)} %get-tuple-element.1640, f32[2,128,1536]{2,0,1:T(2,128)} %copy.152, ...), kind=kLoop, calls=%fused_computation.85 | loop fusion | flops 100188160 | bytes 30916608 | tf_op jit(solution)/shard_map/transpose(jvp())/reduce_sum | solution.py:121
  802.1 32.4 %all_gather.82 = bf16[8,2,16,1536]{3,2,1,0:T(8,128)(2,1)S(1)} all-gather(bf16[1,2,16,1536]{3,2,1,0:T(8,128)(2,1)S(1)} %fusion.118), channel_id=1, replica_groups=mesh['batch'=4,'seq'=8] {'seq'}, dimensions={0}, use_global_device_ids=true | all-gather | bytes 884736 | tf_op jit(solution)/shard_map/all_gather | solution.py:46
  845.8 554.0 %while.201 = (s32[]{:T(128)}, f32[16,1536]{1,0:T(8,128)S(1)}, f32[2,16,1536]{2,1,0:T(8,128)S(1)}, f32[8,16,2,1536]{3,1,0,2:T(8,128)}, f32[8,16,2,1536]{3,1,0,2:T...) while((s32[]{:T(128)}, f32[16,1536]{1,0:T(8,128)S(1)}, ...), condition=%wide.region_30.31_spmd.clone, body=%wide.region_20.30_spmd.clone.sunk | while | flops 1066442 | bytes 7687363 | solution.py:115
  876.6 36.9 %while.204 = (s32[]{:T(128)}, f32[16,1536]{1,0:T(8,128)S(1)}, f32[2,16,1536]{2,1,0:T(8,128)S(1)}, f32[16,2,1536]{2,1,0:T(2,128)S(1)}, f32[16,2,1536]{2,1,0:T(2,1...) while((s32[]{:T(128)}, f32[16,1536]{1,0:T(8,128)S(1)}, ...), condition=%wide.region_29.29_spmd.clone, body=%wide.region_23.28_spmd.clone.sunk | while | flops 764868 | bytes 2080951 | solution.py:112
  945.8 36.9 %while.204 = (s32[]{:T(128)}, f32[16,1536]{1,0:T(8,128)S(1)}, f32[2,16,1536]{2,1,0:T(8,128)S(1)}, f32[16,2,1536]{2,1,0:T(2,128)S(1)}, f32[16,2,1536]{2,1,0:T(2,1...) while((s32[]{:T(128)}, f32[16,1536]{1,0:T(8,128)S(1)}, ...), condition=%wide.region_29.29_spmd.clone, body=%wide.region_23.28_spmd.clone.sunk | while | flops 764868 | bytes 2080951 | solution.py:112
  1015.0 36.9 %while.204 = (s32[]{:T(128)}, f32[16,1536]{1,0:T(8,128)S(1)}, f32[2,16,1536]{2,1,0:T(8,128)S(1)}, f32[16,2,1536]{2,1,0:T(2,128)S(1)}, f32[16,2,1536]{2,1,0:T(2,1...) while((s32[]{:T(128)}, f32[16,1536]{1,0:T(8,128)S(1)}, ...), condition=%wide.region_29.29_spmd.clone, body=%wide.region_23.28_spmd.clone.sunk | while | flops 764868 | bytes 2080951 | solution.py:112
  1084.3 36.9 %while.204 = (s32[]{:T(128)}, f32[16,1536]{1,0:T(8,128)S(1)}, f32[2,16,1536]{2,1,0:T(8,128)S(1)}, f32[16,2,1536]{2,1,0:T(2,128)S(1)}, f32[16,2,1536]{2,1,0:T(2,1...) while((s32[]{:T(128)}, f32[16,1536]{1,0:T(8,128)S(1)}, ...), condition=%wide.region_29.29_spmd.clone, body=%wide.region_23.28_spmd.clone.sunk | while | flops 764868 | bytes 2080951 | solution.py:112
  1153.5 36.9 %while.204 = (s32[]{:T(128)}, f32[16,1536]{1,0:T(8,128)S(1)}, f32[2,16,1536]{2,1,0:T(8,128)S(1)}, f32[16,2,1536]{2,1,0:T(2,128)S(1)}, f32[16,2,1536]{2,1,0:T(2,1...) while((s32[]{:T(128)}, f32[16,1536]{1,0:T(8,128)S(1)}, ...), condition=%wide.region_29.29_spmd.clone, body=%wide.region_23.28_spmd.clone.sunk | while | flops 764868 | bytes 2080951 | solution.py:112
  1222.8 36.9 %while.204 = (s32[]{:T(128)}, f32[16,1536]{1,0:T(8,128)S(1)}, f32[2,16,1536]{2,1,0:T(8,128)S(1)}, f32[16,2,1536]{2,1,0:T(2,128)S(1)}, f32[16,2,1536]{2,1,0:T(2,1...) while((s32[]{:T(128)}, f32[16,1536]{1,0:T(8,128)S(1)}, ...), condition=%wide.region_29.29_spmd.clone, body=%wide.region_23.28_spmd.clone.sunk | while | flops 764868 | bytes 2080951 | solution.py:112
  1292.1 36.9 %while.204 = (s32[]{:T(128)}, f32[16,1536]{1,0:T(8,128)S(1)}, f32[2,16,1536]{2,1,0:T(8,128)S(1)}, f32[16,2,1536]{2,1,0:T(2,128)S(1)}, f32[16,2,1536]{2,1,0:T(2,1...) while((s32[]{:T(128)}, f32[16,1536]{1,0:T(8,128)S(1)}, ...), condition=%wide.region_29.29_spmd.clone, body=%wide.region_23.28_spmd.clone.sunk | while | flops 764868 | bytes 2080951 | solution.py:112
  1361.3 36.9 %while.204 = (s32[]{:T(128)}, f32[16,1536]{1,0:T(8,128)S(1)}, f32[2,16,1536]{2,1,0:T(8,128)S(1)}, f32[16,2,1536]{2,1,0:T(2,128)S(1)}, f32[16,2,1536]{2,1,0:T(2,1...) while((s32[]{:T(128)}, f32[16,1536]{1,0:T(8,128)S(1)}, ...), condition=%wide.region_29.29_spmd.clone, body=%wide.region_23.28_spmd.clone.sunk | while | flops 764868 | bytes 2080951 | solution.py:112
  1404.6 25.1 %multiply_reduce_fusion.5 = (f32[16,1536]{1,0:T(8,128)}, f32[2,128,1536]{2,0,1:T(2,128)S(1)}) fusion(f32[2,1,16,1536]{3,2,0,1:T(8,128)} %multiply_bitcast_fusion, f32[2,16,1536]{2,1,0:T(8,128)S(1)} %get-tuple-element.1128, f32[2,128,16]{2,0,1:T(2,128)} %copy.149, f32[2,128,1536]{2,0,1:T(2,128)} %copy.148, f32[16,1536]{1,0:T(8,128)S(1)} %get-tuple-element.2595), kind=kLoop, calls=%fused_computation.84 | loop fusion | flops 56205312 | bytes 3751936 | tf_op jit(solution)/shard_map/transpose(jvp())/reduce_sum | solution.py:121
  1433.0 28.9 %reduce_window_sum.30 = f32[2,128,1536]{2,1,0:T(8,128)} reduce-window(f32[2,128,1536]{2,1,0:T(8,128)} %copy.160, f32[]{:T(128)} %constant.324.clone.1), window={size=1x128x1 pad=0_0x0_127x0_0}, to_apply=%region_34.35 | reduce-window | flops 49938432 | bytes 3145732 | tf_op jit(solution)/shard_map/transpose(jvp(jit(cumsum)))/reduce_window_sum | solution.py:121
  1461.9 28.8 %reduce_window_sum.29 = f32[2,128,1536]{2,1,0:T(8,128)} reduce-window(f32[2,128,1536]{2,1,0:T(8,128)} %copy.159, f32[]{:T(128)} %constant.324.clone.1), window={size=1x128x1 pad=0_0x0_127x0_0}, to_apply=%region_32.33 | reduce-window | flops 49938432 | bytes 3145732 | tf_op jit(solution)/shard_map/transpose(jvp(jit(cumsum)))/reduce_window_sum | solution.py:121
  1553.0 37.8 %all-reduce.21 = (f32[1536]{0:T(1024)S(1)}, f32[1536]{0:T(1024)S(1)}, f32[1536]{0:T(1024)S(1)}, f32[768]{0:T(1024)S(1)}, f32[768]{0:T(1024)S(1)}, /*index=5*/f32[768,8]{0,1:T(8,128)S(1)}) all-reduce(f32[1536]{0:T(1024)S(1)} %get-tuple-element.1428, ...), channel_id=5, replica_groups=mesh['batch'=4,'seq'=8] {'batch','seq'}, use_global_device_ids=true, to_apply=%region_45.46.clone | all-reduce | flops 12288 | bytes 98304
  1596.9 96.7 %reduce-scatter.30.cloned.1.call-done = f32[48,16]{1,0:T(8,128)} async-done(((f32[1536,16]{1,0:T(8,128)}), f32[48,16]{1,0:T(8,128)}) %reduce-scatter.30.cloned.1.call-update) | async-done | bytes 3088
  1695.0 98.2 %reduce-scatter.28.cloned.1.call-done = f32[48,48]{1,0:T(8,128)} async-done(((f32[1536,48]{1,0:T(8,128)}), f32[48,48]{1,0:T(8,128)}) %reduce-scatter.28.cloned.1.call-update) | async-done | bytes 9232
  1794.7 48.0 %reduce-scatter.22.cloned.1.call-done = bf16[1,768,768]{2,1,0:T(8,128)(2,1)} async-done(((bf16[1,768,3072]{2,1,0:T(8,128)(2,1)}), bf16[1,768,768]{2,1,0:T(8,128)(2,1)}) %reduce-scatter.22.cloned.1.call-update) | async-done | bytes 1179664 | tf_op jit(solution)/shard_map/reduce_scatter | solution.py:335
  1845.6 47.7 %reduce-scatter.24.cloned.1.call-done = bf16[1,768,768]{2,1,0:T(8,128)(2,1)} async-done(((bf16[1,3072,768]{2,1,0:T(8,128)(2,1)}), bf16[1,768,768]{2,1,0:T(8,128)(2,1)}) %reduce-scatter.24.cloned.1.call-update) | async-done | bytes 1179664 | tf_op jit(solution)/shard_map/reduce_scatter | solution.py:338
  1896.1 98.2 %reduce-scatter.18.cloned.1.call-done = f32[48,80]{1,0:T(8,128)} async-done(((f32[1536,80]{1,0:T(8,128)}), f32[48,80]{1,0:T(8,128)}) %reduce-scatter.18.cloned.1.call-update) | async-done | bytes 15376 | tf_op jit(solution)/shard_map/reduce_scatter | solution.py:430
  1994.3 112.1 %reduce-scatter.20.cloned.1.call-done = f32[48,768]{1,0:T(8,128)} async-done(((f32[1536,768]{1,0:T(8,128)}), f32[48,768]{1,0:T(8,128)}) %reduce-scatter.20.cloned.1.call-update) | async-done | bytes 147472 | tf_op jit(solution)/shard_map/reduce_scatter | solution.py:435
  2106.4 142.0 %reduce-scatter.16.cloned.1.call-done = f32[24,3072]{1,0:T(8,128)} async-done(((f32[768,3072]{1,0:T(8,128)}), f32[24,3072]{1,0:T(8,128)}) %reduce-scatter.16.cloned.1.call-update) | async-done | bytes 294928 | tf_op jit(solution)/shard_map/reduce_scatter | solution.py:427
  (3174 shorter events, 1142.7 us)
Async XLA Ops:
  7.2 252.4 %copy-start.16 = (bf16[2,128,768]{2,1,0:T(8,128)(2,1)S(1)}, bf16[2,128,768]{2,1,0:T(8,128)(2,1)}, u32[]{:S(2)}) copy-start(bf16[2,128,768]{2,1,0:T(8,128)(2,1)} %param.34) | copy-start | bytes 1179652
  7.2 252.3 %copy-start.81 = (s32[2,128]{1,0:T(2,128)S(1)}, s32[2,128]{1,0:T(2,128)}, u32[]{:S(2)}) copy-start(s32[2,128]{1,0:T(2,128)} %param.50) | copy-start | bytes 3076
  7.2 252.3 %copy-start.73 = (s32[2,128]{1,0:T(2,128)S(1)}, s32[2,128]{1,0:T(2,128)}, u32[]{:S(2)}) copy-start(s32[2,128]{1,0:T(2,128)} %param.49) | copy-start | bytes 3076
  7.2 252.4 %all-gather.9.cloned.1.call-start = ((), (), s32[]{:S(2)}) async-start(), calls=%async_computation.12 | async-start | bytes 4866048 | tf_op jit(solution)/shard_map/all_gather | solution.py:148
  7.9 499.5 %all-gather.11.cloned.1.call-start = ((), (), s32[]{:S(2)}) async-start(), calls=%async_computation.13 | async-start | bytes 2433024 | tf_op jit(solution)/shard_map/all_gather | solution.py:156
  8.7 543.6 %all-gather.13.cloned.1.call-start = ((), (), s32[]{:S(2)}) async-start(), calls=%async_computation.14 | async-start | bytes 5898240 | tf_op jit(solution)/shard_map/all_gather | solution.py:163
  9.4 558.8 %all-gather.15.cloned.1.call-start = ((), (), s32[]{:S(2)}) async-start(), calls=%async_computation.15 | async-start | bytes 5898240 | tf_op jit(solution)/shard_map/all_gather | solution.py:164
  56.8 206.6 %copy-start.39 = (f32[768]{0:T(1024)}, f32[768]{0:T(1024)S(1)}, u32[]{:S(2)}) copy-start(f32[768]{0:T(1024)S(1)} %convert_element_type.194) | copy-start | bytes 9220
  58.6 204.9 %copy-start.53 = (f32[2,128]{1,0:T(2,128)}, f32[2,128]{1,0:T(2,128)S(1)}, u32[]{:S(2)}) copy-start(f32[2,128]{1,0:T(2,128)S(1)} %get-tuple-element.1647) | copy-start | bytes 3076
  124.9 209.8 %copy-start.57 = (f32[1536]{0:T(1024)}, f32[1536]{0:T(1024)S(1)}, u32[]{:S(2)}) copy-start(f32[1536]{0:T(1024)S(1)} %get-tuple-element.1432) | copy-start | bytes 18436
  124.9 209.8 %copy-start.59 = (f32[1536]{0:T(1024)}, f32[1536]{0:T(1024)S(1)}, u32[]{:S(2)}) copy-start(f32[1536]{0:T(1024)S(1)} %get-tuple-element.1433) | copy-start | bytes 18436
  124.9 209.8 %copy-start.61 = (f32[1536]{0:T(1024)}, f32[1536]{0:T(1024)S(1)}, u32[]{:S(2)}) copy-start(f32[1536]{0:T(1024)S(1)} %get-tuple-element.1434) | copy-start | bytes 18436
  124.9 209.8 %copy-start.63 = (f32[1536]{0:T(1024)}, f32[1536]{0:T(1024)S(1)}, u32[]{:S(2)}) copy-start(f32[1536]{0:T(1024)S(1)} %get-tuple-element.1435) | copy-start | bytes 18436
  192.7 144.2 %copy-start.38 = (bf16[1536,80]{1,0:T(8,128)(2,1)}, bf16[1536,80]{1,0:T(8,128)(2,1)S(1)}, u32[]{:S(2)}) copy-start(bf16[1536,80]{1,0:T(8,128)(2,1)S(1)} %all_gather.69) | copy-start | bytes 737284
  265.1 69.5 %collective-permute-start = (bf16[2,3,1536]{2,1,0:T(4,128)(2,1)S(1)}, bf16[2,3,1536]{2,1,0:T(4,128)(2,1)S(1)}, u32[]{:S(2)}, u32[]{:S(2)}) collective-permute-start(bf16[2,3,1536]{2,1,0:T(4,128)(2,1)S(1)} %slice.175), channel_id=1, source_target_pairs={{0,1},{1,2},{2,3},{3,4},{4,5},{5,6},{6,7},{8,9},{9,10},{10,11},{11... | collective-permute-start | bytes 55304 | tf_op jit(solution)/shard_map/ppermute | solution.py:15
  332.8 172.6 %copy-start.70 = (f32[1536]{0:T(1024)}, f32[1536]{0:T(1024)S(1)}, u32[]{:S(2)}) copy-start(f32[1536]{0:T(1024)S(1)} %convert_element_type.202) | copy-start | bytes 18436
  510.3 235.2 %copy-start.6 = (f32[2,128,768]{2,1,0:T(8,128)}, f32[2,128,768]{2,1,0:T(8,128)S(1)}, u32[]{:S(2)}) copy-start(f32[2,128,768]{2,1,0:T(8,128)S(1)} %get-tuple-element.1653) | copy-start | bytes 2359300
  547.8 14.3 all-to-all-start
  568.3 87.4 %copy-start.22 = (bf16[256,768]{1,0:T(8,128)(2,1)S(1)}, bf16[256,768]{1,0:T(8,128)(2,1)}, u32[]{:S(2)}) copy-start(bf16[256,768]{1,0:T(8,128)(2,1)} %multiply_convert_fusion.1) | copy-start | bytes 1179652
  581.3 75.9 %all-to-all-start.1 = ((bf16[8,40,768]{2,1,0:T(8,128)(2,1)}), bf16[8,40,768]{2,1,0:T(8,128)(2,1)S(1)}, u32[]{:S(2)}, u32[]{:S(2)}) async-start(bf16[8,40,768]{2,1,0:T(8,128)(2,1)} %fusion.83), calls=%async_computation.1 | async-start | bytes 983040 | tf_op jit(solution)/shard_map/all_to_all | solution.py:262
  723.0 17.1 all-to-all-start.3
  726.7 868.8 %reduce-scatter.26.cloned.1.call-start = ((), (), s32[]{:S(2)}) async-start(), calls=%async_computation.21 | async-start | bytes 811008
  1433.0 57.8 %copy-start.1 = (f32[2,128,1536]{2,1,0:T(8,128)S(1)}, f32[2,128,1536]{2,1,0:T(8,128)}, u32[]{:S(2)}) copy-start(f32[2,128,1536]{2,1,0:T(8,128)} %copy-done) | copy-start | bytes 4718596
  1502.6 191.0 %reduce-scatter.30.cloned.1.call-start = ((), (), s32[]{:S(2)}) async-start(), calls=%async_computation.23 | async-start | bytes 811008
  1503.9 289.4 %reduce-scatter.28.cloned.1.call-start = ((), (), s32[]{:S(2)}) async-start(), calls=%async_computation.22 | async-start | bytes 811008
  1505.4 337.3 %reduce-scatter.22.cloned.1.call-start = ((), (), s32[]{:S(2)}) async-start(), calls=%async_computation.19 | async-start | bytes 5898240 | tf_op jit(solution)/shard_map/reduce_scatter | solution.py:335
  1511.4 381.9 %reduce-scatter.24.cloned.1.call-start = ((), (), s32[]{:S(2)}) async-start(), calls=%async_computation.20 | async-start | bytes 5898240 | tf_op jit(solution)/shard_map/reduce_scatter | solution.py:338
  1525.8 468.5 %reduce-scatter.18.cloned.1.call-start = ((), (), s32[]{:S(2)}) async-start(), calls=%async_computation.17 | async-start | bytes 811008 | tf_op jit(solution)/shard_map/reduce_scatter | solution.py:430
  1527.8 578.6 %reduce-scatter.20.cloned.1.call-start = ((), (), s32[]{:S(2)}) async-start(), calls=%async_computation.18 | async-start | bytes 4866048 | tf_op jit(solution)/shard_map/reduce_scatter | solution.py:435
  1531.0 717.4 %reduce-scatter.16.cloned.1.call-start = ((), (), s32[]{:S(2)}) async-start(), calls=%async_computation.16 | async-start | bytes 9732096 | tf_op jit(solution)/shard_map/reduce_scatter | solution.py:427
  1534.8 5.7 collective-permute-start.1
  1548.6 45.8 %copy-start.83 = (f32[2,128]{1,0:T(2,128)S(1)}, f32[2,128]{1,0:T(2,128)}, u32[]{:S(2)}) copy-start(f32[2,128]{1,0:T(2,128)} %get-tuple-element.1646) | copy-start | bytes 3076
  (78 other events, 606.1 us)
Sparse Core Ops, SparseCore 0:
  11.0 66.4 all-gather.8
  80.4 56.6 all-gather.10
  138.7 36.2 all-gather.12
  176.4 37.4 all-gather.14
  1502.7 91.3 reduce-scatter.25
  1599.1 94.5 reduce-scatter.29
  1698.7 94.4 reduce-scatter.27
  1795.8 46.8 reduce-scatter.21
  1845.4 47.8 reduce-scatter.23
  1898.8 95.4 reduce-scatter.17
  2000.4 106.0 reduce-scatter.19
  2113.8 134.5 reduce-scatter.15
where the time goes:
time: 2290 us; the launch traced here: 2260 us
  waiting for transfers between devices  670 us (29%)
  other arithmetic  608 us (27%)
  blocking collectives  529 us (23%)
  local copies, waits for them, and re-layouts  312 us (14%)
  matrix products  88.7 us (4%)
    unnamed x15, waiting for transfers between devices  198 us
    dynamic_update_slice x384, other arithmetic, through_block(): return lax.scan(partial(advance, decay_rates), running, block)  192 us
    reduce_sum x128, other arithmetic, advance(): now_b[:, :, None] * (now_dt * now_u)[:, None, :]  176 us
    reduce_scatter x1, waiting for transfers between devices, body(): lax.psum_scatter(grad_in_proj, ('batch', 'seq'), scatter_dimension=0, til...  142 us
    reduce_scatter x1, waiting for transfers between devices, body(): lax.psum_scatter(grad_out_proj, ('batch', 'seq'), scatter_dimension=0, ti...  112 us
    reduce_scatter x1, waiting for transfers between devices, body(): lax.psum_scatter(grad_state_proj, ('batch', 'seq'), scatter_dimension=0,...  98.2 us
    mul x384, local copies, waits for them, and re-layouts, advance(): now_b[:, :, None] * (now_dt * now_u)[:, None, :]  95.8 us
    unnamed x2, blocking collectives  80.4 us
  transfers between devices with their start and end apart: 17, of which 10 were waited for; matrix products, arithmetic and copies ran while one was open for 10% of the time, Pallas kernels for 0%

commit v1 on v0

v1 whole, which is shorter than its diff:
```python
from functools import partial
import functools
import math

import jax
import jax.numpy as jnp
from jax import lax
from jax.experimental import pallas as pl
from jax.experimental.pallas import tpu as pltpu
from jax.sharding import PartitionSpec as P

epsilon = 1e-05
MESH = pl.DeviceIdType.MESH
HBM = pl.BlockSpec(memory_space=pl.ANY)
VM = pl.BlockSpec(memory_space=pltpu.VMEM)
bf16, f32 = jnp.bfloat16, jnp.float32


class Place:
    def __init__(self, batch, seq, ydim=2):
        self.batch, self.seq, self.Y = batch, seq, ydim
        self.Z = seq // ydim
        b, s = lax.axis_index("batch"), lax.axis_index("seq")
        self.x, self.c = b // 2, b % 2
        self.z, self.y = s // ydim, s % ydim

    def at(self, x=None, c=None, y=None, z=None):
        pick = lambda v, own: own if v is None else v
        x, c, y, z = pick(x, self.x), pick(c, self.c), pick(y, self.y), pick(z, self.z)
        return (x * 2 + c, z * self.Y + y)

    def index(self, dev):
        return dev[0] * self.seq + dev[1]


def greet(devices):
    barrier = pltpu.get_barrier_semaphore()
    count = 0
    for pred, dev in devices:
        if pred is None:
            pl.semaphore_signal(barrier, inc=1, device_id=dev, device_id_type=MESH)
            count = count + 1
        else:
            @pl.when(pred)
            def _(dev=dev):
                pl.semaphore_signal(barrier, inc=1, device_id=dev, device_id_type=MESH)
            count = count + jnp.where(pred, 1, 0)
    pl.semaphore_wait(barrier, count)


def gather_kernel(batch, seq, n_arrays, *refs):
    ins, outs = refs[:n_arrays], refs[n_arrays : 2 * n_arrays]
    local_sem, send_sem, recv_sem = refs[2 * n_arrays :]
    me = Place(batch, seq)
    Z, z = me.Z, me.z
    rows = [r.shape[0] for r in ins]
    sib = me.at(c=1 - me.c)
    up_ok, down_ok = z < Z - 1, z > 0
    up, down = me.at(z=z + 1), me.at(z=z - 1)
    nx, ny = me.at(x=1 - me.x), me.at(y=1 - me.y)
    first = me.c == 0
    nb2 = tuple(jnp.where(first, a, b) for a, b in zip(ny, nx))
    nb3 = tuple(jnp.where(first, a, b) for a, b in zip(nx, ny))
    x2, y2 = jnp.where(first, me.x, 1 - me.x), jnp.where(first, 1 - me.y, me.y)
    x3, y3 = jnp.where(first, 1 - me.x, me.x), jnp.where(first, me.y, 1 - me.y)
    greet([(None, sib), (None, nx), (None, ny), (up_ok, up), (down_ok, down)])
    own = me.index(me.at())

    def part(a, index):
        return outs[a].at[pl.ds(pl.multiple_of(index * rows[a], 8), rows[a])]

    sends = []

    def send(pred, index, dev, mine=False):
        slot = len(sends)
        copies = []
        for a in range(n_arrays):
            copies.append(
                pltpu.make_async_remote_copy(
                    src_ref=ins[a] if mine else part(a, index),
                    dst_ref=part(a, index),
                    send_sem=send_sem.at[slot, a],
                    recv_sem=recv_sem.at[index, a],
                    device_id=dev,
                    device_id_type=MESH,
                )
            )

        def go():
            for cp in copies:
                cp.start()
        if pred is None:
            go()
        else:
            pl.when(pred)(go)
        sends.append((pred, copies))

    def arrive(pred, index, targets):
        def wait():
            for a in range(n_arrays):
                pltpu.make_async_remote_copy(
                    src_ref=part(a, index), dst_ref=part(a, index),
                    send_sem=send_sem.at[0, a], recv_sem=recv_sem.at[index, a],
                    device_id=sib, device_id_type=MESH,
                ).wait_recv()
        if pred is None:
            wait()
        else:
            pl.when(pred)(wait)
        for extra, dev in targets:
            p = pred if extra is None else (extra if pred is None else jnp.logical_and(pred, extra))
            send(p, index, dev)

    for dev, pred in ((up, up_ok), (down, down_ok), (nb2, None), (nb3, None), (sib, None)):
        send(pred, own, dev, mine=True)
    local = [pltpu.make_async_copy(ins[a], part(a, own), local_sem.at[a]) for a in range(n_arrays)]
    for cp in local:
        cp.start()

    def offsets(k):
        return [(None, 0)] if k == 0 else [(z >= k, -k), (z + k < Z, k)]

    def col(k):
        for pred, off in offsets(k):
            fwd = (up_ok, up) if off < 0 else (down_ok, down)
            arrive(pred, me.index(me.at(z=z + off)), [fwd, (None, nb2), (None, nb3), (None, sib)])

    def second(k):
        for pred, off in offsets(k):
            arrive(pred, me.index(me.at(x=x2, y=y2, z=z + off)), [(None, nb3), (None, sib)])

    def third(k):
        for pred, off in offsets(k):
            arrive(pred, me.index(me.at(x=x3, y=y3, z=z + off)), [(None, sib)])

    def fourth(k):
        for pred, off in offsets(k):
            arrive(pred, me.index(me.at(x=1 - me.x, y=1 - me.y, z=z + off)), [(None, sib)])

    for h in range(1, Z + 3):
        if h < Z:
            col(h)
        if 0 <= h - 1 < Z:
            second(h - 1)
        if 0 <= h - 2 < Z:
            third(h - 2)
        if 0 <= h - 3 < Z:
            fourth(h - 3)
    for h in range(Z):
        for xx in (0, 1):
            for yy in (0, 1):
                for pred, off in offsets(h):
                    arrive(pred, me.index(me.at(x=xx, y=yy, c=1 - me.c, z=z + off)), [])
    for cp in local:
        cp.wait()
    for pred, copies in sends:
        def done(copies=copies):
            for cp in copies:
                cp.wait_send()
        if pred is None:
            done()
        else:
            pl.when(pred)(done)


def n_sends(Z):
    return 5 + (Z - 1) * 8 + (2 * Z - 1) * 2 + (2 * Z - 1) * 2


def gather_all(batch, seq, *shards):
    n, count = len(shards), batch * seq
    return pl.pallas_call(
        functools.partial(gather_kernel, batch, seq, n),
        out_shape=[jax.ShapeDtypeStruct((count * a.shape[0],) + a.shape[1:], a.dtype) for a in shards],
        in_specs=[HBM] * n,
        out_specs=[HBM] * n,
        scratch_shapes=[
            pltpu.SemaphoreType.DMA((n,)),
            pltpu.SemaphoreType.DMA((n_sends(seq // 2), n)),
            pltpu.SemaphoreType.DMA((count, n)),
        ],
        compiler_params=pltpu.CompilerParams(collective_id=0, has_side_effects=True),
        name="gather_weights",
    )(*shards)


def reduce_kernel(batch, seq, n_arrays, *refs):
    n = n_arrays
    ins, outs = refs[:n], refs[n : 2 * n]
    work, sib_buf, far_buf, near_buf, line_buf = (refs[(2 + i) * n : (3 + i) * n] for i in range(5))
    load_sem, send_sem, sib_sem, far_sem, near_sem, line_sem = refs[7 * n :]
    me = Place(batch, seq)
    Z, z = me.Z, me.z
    rows = [r.shape[0] for r in outs]
    sib = me.at(c=1 - me.c)
    up, down = me.at(z=z + 1), me.at(z=z - 1)
    nx, ny = me.at(x=1 - me.x), me.at(y=1 - me.y)
    first = me.c == 0
    pick = lambda flag, a, b: jnp.where(flag, a, b)
    near = tuple(pick(first, a, b) for a, b in zip(ny, nx))
    far = tuple(pick(first, a, b) for a, b in zip(nx, ny))
    greet([(None, sib), (None, nx), (None, ny), (z < Z - 1, up), (z > 0, down)])

    def groups(c):
        f = c == 0
        ox, oy = 1 - me.x, 1 - me.y
        return [
            (ox, oy),
            (pick(f, ox, me.x), pick(f, me.y, oy)),
            (pick(f, me.x, ox), pick(f, oy, me.y)),
            (me.x, me.y),
        ]

    def slot(xy, zz):
        return (xy[0] * 2 + xy[1]) * Z + zz

    def turn(k):
        return (z + 1 + k) % Z

    sends = []

    def send(pred, srcs, dsts, recv, dev):
        copies = [
            pltpu.make_async_remote_copy(
                src_ref=srcs[a], dst_ref=dsts[a], send_sem=send_sem.at[len(sends), a],
                recv_sem=recv(a), device_id=dev, device_id_type=MESH)
            for a in range(n)
        ]

        def go():
            for cp in copies:
                cp.start()
        if pred is None:
            go()
        else:
            pl.when(pred)(go)
        sends.append((pred, copies))

    def take(bufs, recv):
        for a in range(n):
            pltpu.make_async_remote_copy(
                src_ref=bufs[a], dst_ref=bufs[a], send_sem=send_sem.at[0, a],
                recv_sem=recv(a), device_id=sib, device_id_type=MESH).wait_recv()

    def source(a, c, xy, zz):
        index = me.index((xy[0] * 2 + c, zz * me.Y + xy[1]))
        return ins[a].at[pl.ds(pl.multiple_of(index * rows[a], 8), rows[a])]

    other = 1 - me.c
    for xy in groups(other):
        for k in range(Z):
            s = slot(xy, turn(k))
            send(None, [source(a, other, xy, turn(k)) for a in range(n)],
                 [sib_buf[a].at[s] for a in range(n)], lambda a, s=s: sib_sem.at[s, a], sib)
    mine = groups(me.c)
    loads = []
    for xy in mine:
        for k in range(Z):
            s = slot(xy, turn(k))
            cps = [pltpu.make_async_copy(source(a, me.c, xy, turn(k)), work[a].at[s], load_sem.at[s, a])
                   for a in range(n)]
            for cp in cps:
                cp.start()
            loads.append(cps)

    def total(bufs):
        t = bufs[0][...].astype(jnp.float32)
        for b in bufs[1:]:
            t = t + b[...].astype(jnp.float32)
        return t

    for g, xy in enumerate(mine):
        for k in range(Z):
            zz = turn(k)
            s = slot(xy, zz)
            for cp in loads[g * Z + k]:
                cp.wait()
            take([sib_buf[a].at[s] for a in range(n)], lambda a: sib_sem.at[s, a])
            parts = [[work[a].at[s], sib_buf[a].at[s]] for a in range(n)]
            if g >= 2:
                fs = (g - 2) * Z + zz
                take([far_buf[a].at[fs] for a in range(n)], lambda a: far_sem.at[fs, a])
                for a in range(n):
                    parts[a].append(far_buf[a].at[fs])
            if g == 3:
                take([near_buf[a].at[zz] for a in range(n)], lambda a: near_sem.at[zz, a])
                for a in range(n):
                    parts[a].append(near_buf[a].at[zz])
            if g < 3:
                for a in range(n):
                    work[a][s] = total(parts[a]).astype(jnp.bfloat16)
                srcs = [work[a].at[s] for a in range(n)]
                if g < 2:
                    fs = g * Z + zz
                    send(None, srcs, [far_buf[a].at[fs] for a in range(n)],
                         lambda a: far_sem.at[fs, a], far)
                else:
                    send(None, srcs, [near_buf[a].at[zz] for a in range(n)],
                         lambda a: near_sem.at[zz, a], near)
                continue
            if k < Z - 1:
                rising = zz > z
                side = jnp.where(rising, 0, 1)
                more = jnp.where(rising, z, Z - 1 - z) > 0
                line = [line_buf[a].at[side, zz] for a in range(n)]
                for a in range(n):
                    work[a][s] = total(parts[a]).astype(jnp.bfloat16)

                @pl.when(more)
                def _():
                    take(line, lambda a: line_sem.at[side, zz, a])
                    for a in range(n):
                        work[a][s] = total([work[a].at[s], line[a]]).astype(jnp.bfloat16)
                dev = (me.at()[0], jnp.where(rising, up[1], down[1]))
                send(None, [work[a].at[s] for a in range(n)], line,
                     lambda a: line_sem.at[side, zz, a], dev)
            else:
                for a in range(n):
                    outs[a][...] = total(parts[a])
                for side, pred in ((0, z > 0), (1, z < Z - 1)):
                    @pl.when(pred)
                    def _(side=side):
                        line = [line_buf[a].at[side, zz] for a in range(n)]
                        take(line, lambda a: line_sem.at[side, zz, a])
                        for a in range(n):
                            outs[a][...] = outs[a][...] + line[a][...].astype(jnp.float32)
    for pred, copies in sends:
        for cp in copies:
            cp.wait_send()


def reduce_all(batch, seq, *sums):
    n, count, Z = len(sums), batch * seq, seq // 2
    shapes = [(a.shape[0] // count,) + a.shape[1:] for a in sums]
    half = count // 2
    scratch = []
    for lead in ((half,), (half,), (2 * Z,), (Z,), (2, Z)):
        scratch += [pltpu.VMEM(lead + s, jnp.bfloat16) for s in shapes]
    n_send = half + 2 * Z + Z + Z
    scratch += [
        pltpu.SemaphoreType.DMA((half, n)),
        pltpu.SemaphoreType.DMA((n_send, n)),
        pltpu.SemaphoreType.DMA((half, n)),
        pltpu.SemaphoreType.DMA((2 * Z, n)),
        pltpu.SemaphoreType.DMA((Z, n)),
        pltpu.SemaphoreType.DMA((2, Z, n)),
    ]
    return pl.pallas_call(
        functools.partial(reduce_kernel, batch, seq, n),
        out_shape=[jax.ShapeDtypeStruct(s, jnp.float32) for s in shapes],
        in_specs=[HBM] * n,
        out_specs=[pl.BlockSpec(memory_space=pltpu.VMEM)] * n,
        scratch_shapes=scratch,
        compiler_params=pltpu.CompilerParams(
            collective_id=1, has_side_effects=True, vmem_limit_bytes=40 << 20),
        name="reduce_grads",
    )(*sums)


def spread_kernel(batch, seq, rows_ref, out_ref, local_sem, send_sem, recv_sem):
    me = Place(batch, seq)
    b, s = me.at()
    sib, nx = me.at(c=1 - me.c), me.at(x=1 - me.x)
    greet([(None, sib), (None, nx)] + [(None, (b, (s + k) % seq)) for k in range(1, seq)])
    sends = []

    def send(src, dst, recv, dev):
        cp = pltpu.make_async_remote_copy(
            src_ref=src, dst_ref=dst, send_sem=send_sem.at[len(sends)], recv_sem=recv,
            device_id=dev, device_id_type=MESH)
        cp.start()
        sends.append(cp)

    def arrived(bb, ss):
        pltpu.make_async_remote_copy(
            src_ref=out_ref.at[bb, ss], dst_ref=out_ref.at[bb, ss], send_sem=send_sem.at[0],
            recv_sem=recv_sem.at[bb, ss], device_id=sib, device_id_type=MESH).wait_recv()

    for k in range(seq - 1, 0, -1):
        there = (s + k) % seq
        send(rows_ref.at[there], out_ref.at[b, s], recv_sem.at[b, s], (b, there))
    for dev in (nx, sib):
        send(rows_ref.at[s], out_ref.at[b, s], recv_sem.at[b, s], dev)
    local = pltpu.make_async_copy(rows_ref.at[s], out_ref.at[b, s], local_sem)
    local.start()
    near = nx[0]
    for k in range(1, seq):
        there = (s + k) % seq
        arrived(b, there)
        for dev in (nx, sib):
            send(out_ref.at[b, there], out_ref.at[b, there], recv_sem.at[b, there], dev)
        there = (s + k - 1) % seq
        arrived(near, there)
        send(out_ref.at[near, there], out_ref.at[near, there], recv_sem.at[near, there], sib)
    there = (s + seq - 1) % seq
    arrived(near, there)
    send(out_ref.at[near, there], out_ref.at[near, there], recv_sem.at[near, there], sib)
    for k in range(seq):
        there = (s + k) % seq
        arrived(sib[0], there)
        arrived((1 - me.x) * 2 + 1 - me.c, there)
    local.wait()
    for cp in sends:
        cp.wait_send()


def spread_rows(batch, seq, rows):
    if not tuned(batch, seq):
        mine = lax.all_to_all(rows, "seq", split_axis=0, concat_axis=0, tiled=True)
        return lax.all_gather(mine, "batch", axis=0)
    return pl.pallas_call(
        functools.partial(spread_kernel, batch, seq),
        out_shape=jax.ShapeDtypeStruct((batch,) + rows.shape, rows.dtype),
        in_specs=[HBM],
        out_specs=HBM,
        scratch_shapes=[
            pltpu.SemaphoreType.DMA,
            pltpu.SemaphoreType.DMA((seq - 1 + 2 * seq + seq,)),
            pltpu.SemaphoreType.DMA((batch, seq)),
        ],
        compiler_params=pltpu.CompilerParams(collective_id=2, has_side_effects=True),
        name="spread_rows",
    )(rows)


def tuned(batch, seq):
    return batch == 4 and seq == 8


def collect_kernel(batch, seq, part_ref, out_ref, held, total, sib_buf, near_buf,
                   load_sem, send_sem, sib_sem, near_sem, out_sem, local_sem):
    me = Place(batch, seq)
    b, s = me.at()
    sib, nx = me.at(c=1 - me.c), me.at(x=1 - me.x)
    greet([(None, sib), (None, nx)] + [(None, (b, (s + k) % seq)) for k in range(1, seq)])
    sends = []

    def send(src, dst, recv, dev):
        cp = pltpu.make_async_remote_copy(
            src_ref=src, dst_ref=dst, send_sem=send_sem.at[len(sends)], recv_sem=recv,
            device_id=dev, device_id_type=MESH)
        cp.start()
        sends.append(cp)

    def arrived(ref, recv):
        pltpu.make_async_remote_copy(
            src_ref=ref, dst_ref=ref, send_sem=send_sem.at[0],
            recv_sem=recv, device_id=sib, device_id_type=MESH).wait_recv()

    f32 = lambda ref: ref[...].astype(jnp.float32)
    far_x = 1 - me.x
    turn = lambda k: (s + 1 + k) % seq
    loads = []
    for k in range(seq):
        t = turn(k)
        for g, xx in enumerate((far_x, me.x)):
            send(part_ref.at[xx * 2 + 1 - me.c, t], sib_buf.at[g, t], sib_sem.at[g, t], sib)
            cp = pltpu.make_async_copy(part_ref.at[xx * 2 + me.c, t], held.at[g, t], load_sem.at[g, t])
            cp.start()
            loads.append(cp)

    def first(k):
        t = turn(k)
        loads[2 * k].wait()
        arrived(sib_buf.at[0, t], sib_sem.at[0, t])
        total[0, t] = (f32(held.at[0, t]) + f32(sib_buf.at[0, t])).astype(jnp.bfloat16)
        send(total.at[0, t], near_buf.at[t], near_sem.at[t], nx)

    def second(k):
        t = turn(k)
        loads[2 * k + 1].wait()
        arrived(sib_buf.at[1, t], sib_sem.at[1, t])
        arrived(near_buf.at[t], near_sem.at[t])
        total[1, t] = (f32(held.at[1, t]) + f32(sib_buf.at[1, t]) + f32(near_buf.at[t])).astype(jnp.bfloat16)
        if k < seq - 1:
            send(total.at[1, t], out_ref.at[s], out_sem.at[s], (b, t))
        else:
            cp = pltpu.make_async_copy(total.at[1, t], out_ref.at[s], local_sem)
            cp.start()
            return cp

    first(0)
    first(1)
    for k in range(seq):
        if k + 2 < seq:
            first(k + 2)
        own = second(k)
    for k in range(1, seq):
        t = (s + k) % seq
        arrived(out_ref.at[t], out_sem.at[t])
    own.wait()
    for cp in sends:
        cp.wait_send()


def collect_rows(batch, seq, part):
    if not tuned(batch, seq):
        mine = lax.psum_scatter(part, "batch", scatter_dimension=0, tiled=False)
        return lax.all_to_all(mine, "seq", split_axis=0, concat_axis=0, tiled=True)
    slab = part.shape[2:]
    return pl.pallas_call(
        functools.partial(collect_kernel, batch, seq),
        out_shape=jax.ShapeDtypeStruct((seq,) + slab, part.dtype),
        in_specs=[HBM],
        out_specs=HBM,
        scratch_shapes=[
            pltpu.VMEM((2, seq) + slab, part.dtype),
            pltpu.VMEM((2, seq) + slab, part.dtype),
            pltpu.VMEM((2, seq) + slab, part.dtype),
            pltpu.VMEM((seq,) + slab, part.dtype),
            pltpu.SemaphoreType.DMA((2, seq)),
            pltpu.SemaphoreType.DMA((4 * seq - 1,)),
            pltpu.SemaphoreType.DMA((2, seq)),
            pltpu.SemaphoreType.DMA((seq,)),
            pltpu.SemaphoreType.DMA((seq,)),
            pltpu.SemaphoreType.DMA,
        ],
        compiler_params=pltpu.CompilerParams(
            collective_id=3, has_side_effects=True, vmem_limit_bytes=32 << 20),
        name="collect_rows",
    )(part)


def chain_kernel(seq, forward, dsum_ref, rates_ref, end_ref, out_ref, held, outgoing, send_sem, recv_sem):
    s = lax.axis_index("seq")
    b = lax.axis_index("batch")
    step = 1 if forward else -1
    has_before = s > 0 if forward else s < seq - 1
    has_after = s < seq - 1 if forward else s > 0
    before, after = (b, s - step), (b, s + step)
    barrier = pltpu.get_barrier_semaphore()
    for pred, dev in ((has_before, before), (has_after, after)):
        @pl.when(pred)
        def _(dev=dev):
            pl.semaphore_signal(barrier, inc=1, device_id=dev, device_id_type=MESH)
    pl.semaphore_wait(barrier, jnp.where(has_before, 1, 0) + jnp.where(has_after, 1, 0))
    count = end_ref.shape[0]

    def copy(i):
        return pltpu.make_async_remote_copy(
            src_ref=outgoing.at[i], dst_ref=held.at[i], send_sem=send_sem.at[i],
            recv_sem=recv_sem.at[i], device_id=after, device_id_type=MESH)

    for i in range(count):
        @pl.when(has_before)
        def _(i=i):
            copy(i).wait_recv()
            out_ref[i] = held[i].astype(jnp.float32)
            decay = jnp.exp(rates_ref[...] * dsum_ref[i])
            outgoing[i] = (end_ref[i] + decay * out_ref[i]).astype(jnp.bfloat16)

        @pl.when(jnp.logical_not(has_before))
        def _(i=i):
            out_ref[i] = jnp.zeros_like(out_ref[i])
            outgoing[i] = end_ref[i].astype(jnp.bfloat16)

        @pl.when(has_after)
        def _(i=i):
            copy(i).start()
    for i in range(count):
        @pl.when(has_after)
        def _(i=i):
            copy(i).wait_send()


def chain_states(seq, forward, dsum, rates, end):
    vm = pl.BlockSpec(memory_space=pltpu.VMEM)
    return pl.pallas_call(
        functools.partial(chain_kernel, seq, forward),
        out_shape=jax.ShapeDtypeStruct(end.shape, jnp.float32),
        in_specs=[vm] * 3,
        out_specs=vm,
        scratch_shapes=[
            pltpu.VMEM(end.shape, jnp.bfloat16),
            pltpu.VMEM(end.shape, jnp.bfloat16),
            pltpu.SemaphoreType.DMA((end.shape[0],)),
            pltpu.SemaphoreType.DMA((end.shape[0],)),
        ],
        compiler_params=pltpu.CompilerParams(
            collective_id=4 if forward else 5, has_side_effects=True),
        name="chain_forward" if forward else "chain_backward",
    )(dsum, rates, end)


def dot(a, b):
    return jnp.dot(a, b, preferred_element_type=jnp.float32)


def dot_nt(a, b):
    return lax.dot_general(a, b, (((1,), (1,)), ((), ())), preferred_element_type=jnp.float32)


def dot_tn(a, b):
    return lax.dot_general(a, b, (((0,), (0,)), ((), ())), preferred_element_type=jnp.float32)


def sigmoid(v):
    return 1.0 / (1.0 + jnp.exp(-v))


def lanes(shape):
    return lax.broadcasted_iota(jnp.int32, shape, 1)


def subs(shape):
    return lax.broadcasted_iota(jnp.int32, shape, 0)


def column(row, base, states):
    shape = (states, row.shape[1])
    only = jnp.where(lanes(shape) == subs(shape) + base, jnp.broadcast_to(row, shape), 0.0)
    return jnp.broadcast_to(jnp.sum(only, axis=1, keepdims=True), shape)


def block_diagonal(rows, base, states):
    t = rows.shape[0]
    pick = (rows.shape[1], t * states)
    spread = (subs(pick) == lanes(pick) % states + base).astype(jnp.bfloat16)
    wide = dot(rows.astype(jnp.bfloat16), spread)
    own = lanes(wide.shape) // states == subs(wide.shape)
    return jnp.where(own, wide, 0.0).astype(jnp.bfloat16)


WIDE = 256
GROUP = 16
LOG2E = math.log2(math.e)


def conv_sum(ext_ref, s, cols, vec_ref, states, taps, rows):
    first = ext_ref.shape[1] - rows - taps + 1
    total = vec_ref[states + taps : states + taps + 1, cols]
    for k in range(taps):
        total = total + vec_ref[states + k : states + k + 1, cols] * ext_ref[s, first + k : first + k + rows, cols]
    return total


def normalize(x):
    return lax.rsqrt(jnp.mean(x * x, axis=-1, keepdims=True) + epsilon)


def enter_kernel(dims, tok_ref, halo_ref, win_ref, small_ref, vec_ref, gain_ref,
                 ext_ref, z_ref, u_ref, dt_ref, proj_ref, end_ref, dsum_ref, xn):
    seqs, rows, inner, states, rank, taps = dims
    count = seqs * rows
    for ref, at in ((tok_ref, 0), (halo_ref, count)):
        x = ref[...].astype(jnp.float32)
        xn[at : at + x.shape[0]] = (x * normalize(x) * gain_ref[0:1]).astype(jnp.bfloat16)
    proj = jnp.zeros((count, small_ref.shape[1]), jnp.float32)
    for j in range(inner // WIDE):
        cols = slice(j * WIDE, (j + 1) * WIDE)
        part = dot(xn[...], win_ref[:, cols])
        z_ref[:, cols] = dot(xn[:count], win_ref[:, inner + j * WIDE : inner + (j + 1) * WIDE])
        for s in range(seqs):
            ext_ref[s, 0:8, cols] = part[count + 8 * s : count + 8 * s + 8]
            ext_ref[s, 8:, cols] = part[s * rows : (s + 1) * rows]
            pre = conv_sum(ext_ref, s, cols, vec_ref, states, taps, rows)
            u_ref[s * rows : (s + 1) * rows, cols] = pre * sigmoid(pre)
        proj = proj + dot(u_ref[:, cols].astype(jnp.bfloat16), small_ref[cols, :])
    proj_ref[...] = proj
    low = rank_lanes(proj, rank, states)
    for j in range(inner // WIDE):
        cols = slice(j * WIDE, (j + 1) * WIDE)
        pre = dot_nt(low, small_ref[cols, :]) + vec_ref[states + taps + 1 : states + taps + 2, cols]
        dt = jnp.maximum(pre, 0.0) + jnp.log1p(jnp.exp(-jnp.abs(pre)))
        dt_ref[:, cols] = dt
        for s in range(seqs):
            dsum_ref[s, 0:1, cols] = jnp.sum(dt[s * rows : (s + 1) * rows], axis=0, keepdims=True)
    a2 = -jnp.exp(vec_ref[0:states]) * LOG2E
    blocks = inner // 128
    for s in range(seqs):
        def eight(i, hs):
            hs = list(hs)
            at = pl.multiple_of(s * rows + i * 8, 8)
            small = proj_ref[pl.ds(at, 8), :]
            bs = [column(small[j : j + 1], rank, states) for j in range(8)]
            for k in range(blocks):
                sl = slice(k * 128, (k + 1) * 128)
                d8 = dt_ref[pl.ds(at, 8), sl]
                w8 = d8 * u_ref[pl.ds(at, 8), sl]
                for j in range(8):
                    hs[k] = jnp.exp2(d8[j : j + 1] * a2[:, sl]) * hs[k] + bs[j] * w8[j : j + 1]
            return tuple(hs)
        zero = jnp.zeros((states, 128), jnp.float32)
        hs = lax.fori_loop(0, rows // 8, eight, (zero,) * blocks)
        for k in range(blocks):
            end_ref[s, :, k * 128 : (k + 1) * 128] = hs[k]


def rank_lanes(proj, rank, states):
    at = rank + 2 * states
    moved = pltpu.roll(proj, at, axis=1)
    return jnp.where(lanes(proj.shape) >= at, moved, 0.0).astype(jnp.bfloat16)


def leave_kernel(dims, capacity, tok_ref, cot_ref, h0_ref, dt_ref, u_ref, z_ref, proj_ref, vec_ref, out_ref,
                 gain_ref, router_ref, route_ref, slot_ref, place_ref,
                 hist_ref, y_ref, hid_ref, gated_ref, moe_ref, gate_ref, rows_ref,
                 hbuf, hcur, sem, sem0):
    seqs, rows, inner, states, rank, taps = dims
    count = seqs * rows
    a2 = -jnp.exp(vec_ref[0:states]) * LOG2E
    blocks = inner // 128
    groups = rows // GROUP
    size = GROUP * states
    firsts = []
    for s in range(seqs):
        hcur[s] = h0_ref[s].astype(jnp.bfloat16)
        cp = pltpu.make_async_copy(hcur.at[s], hist_ref.at[s, pl.ds(0, states)], sem0.at[s])
        cp.start()
        firsts.append(cp)

    def out_copy(s, g, slot):
        at = pl.multiple_of(states + g * size, states)
        return pltpu.make_async_copy(hbuf.at[slot], hist_ref.at[s, pl.ds(at, size)], sem.at[slot])

    for s in range(seqs):
        def group(g, hs):
            hs = list(hs)
            slot = g % 2

            @pl.when(g >= 2)
            def _():
                out_copy(s, g - 2, slot).wait()
            for half in range(GROUP // 8):
                at = pl.multiple_of(s * rows + g * GROUP + half * 8, 8)
                small = proj_ref[pl.ds(at, 8), :]
                bs = [column(small[j : j + 1], rank, states) for j in range(8)]
                for k in range(blocks):
                    sl = slice(k * 128, (k + 1) * 128)
                    d8 = dt_ref[pl.ds(at, 8), sl]
                    w8 = d8 * u_ref[pl.ds(at, 8), sl]
                    for j in range(8):
                        t = half * 8 + j
                        hs[k] = jnp.exp2(d8[j : j + 1] * a2[:, sl]) * hs[k] + bs[j] * w8[j : j + 1]
                        hbuf[slot, t * states : (t + 1) * states, sl] = hs[k].astype(jnp.bfloat16)
            at = pl.multiple_of(s * rows + g * GROUP, GROUP)
            mix = block_diagonal(proj_ref[pl.ds(at, GROUP), :], rank + states, states)
            y_ref[pl.ds(at, GROUP), :] = dot(mix, hbuf[slot])
            out_copy(s, g, slot).start()
            return tuple(hs)
        hs = tuple(h0_ref[s, :, k * 128 : (k + 1) * 128] for k in range(blocks))
        lax.fori_loop(0, groups, group, hs)
        for g in (groups - 2, groups - 1):
            out_copy(s, g, g % 2).wait()
    for cp in firsts:
        cp.wait()
    hid = tok_ref[...].astype(jnp.float32)
    for j in range(inner // WIDE):
        cols = slice(j * WIDE, (j + 1) * WIDE)
        y = y_ref[:, cols] + vec_ref[states + taps + 2 : states + taps + 3, cols] * u_ref[:, cols]
        y_ref[:, cols] = y
        z = z_ref[:, cols]
        gated = (y * (z * sigmoid(z))).astype(jnp.bfloat16)
        gated_ref[:, cols] = gated
        hid = hid + dot(gated, out_ref[cols, :])
    hid_ref[...] = hid
    moe_in = (hid * normalize(hid) * gain_ref[1:2]).astype(jnp.bfloat16)
    moe_ref[...] = moe_in
    logits = dot(moe_in, router_ref[...])
    chosen = lanes(logits.shape) == route_ref[...]
    gate = sigmoid(jnp.sum(jnp.where(chosen, logits, 0.0), axis=1, keepdims=True))
    gate_ref[...] = gate
    kept = (slot_ref[...] < capacity).astype(jnp.float32)
    grad_rows = (cot_ref[...].astype(jnp.float32) * (gate * kept)).astype(jnp.bfloat16)
    total = rows_ref.shape[0]
    pick = (subs((total, count)) == place_ref[...]).astype(jnp.bfloat16)
    width = moe_in.shape[1]
    rows_ref[:, :width] = dot(pick, moe_in).astype(jnp.bfloat16)
    rows_ref[:, width:] = dot(pick, grad_rows).astype(jnp.bfloat16)


def erf(x):
    x = jnp.clip(x, -4.0, 4.0)
    x2 = x * x
    top = (-2.72614225801306e-10, 2.77068142495902e-08, -2.10102402082508e-06, -5.69250639462346e-05,
           -7.34990630326855e-04, -2.95459980854025e-03, -1.60960333262415e-02)
    low = (-1.45660718464996e-05, -2.13374055278905e-04, -1.68282697438203e-03, -7.37332916720468e-03,
           -1.42647390514189e-02)
    p = jnp.full_like(x2, top[0])
    for c in top[1:]:
        p = p * x2 + c
    q = jnp.full_like(x2, low[0])
    for c in low[1:]:
        q = q * x2 + c
    return x * p / q


def expert_kernel(rows_ref, up_ref, down_ref, part_ref, dup_ref, ddown_ref):
    width = up_ref.shape[0]
    x, g = rows_ref[:, :width], rows_ref[:, width:]
    hidden = dot(x, up_ref[...])
    half = 0.5 * (1.0 + erf(hidden * math.sqrt(0.5)))
    act = (hidden * half).astype(jnp.bfloat16)
    slope = half + hidden * (jnp.exp(-0.5 * hidden * hidden) * (1.0 / math.sqrt(2.0 * math.pi)))
    part_ref[:, :width] = dot(act, down_ref[...]).astype(jnp.bfloat16)
    grad_hidden = (dot_nt(g, down_ref[...]) * slope).astype(jnp.bfloat16)
    part_ref[:, width:] = dot_nt(grad_hidden, up_ref[...]).astype(jnp.bfloat16)
    ddown, dup = dot_tn(act, g), dot_tn(x, grad_hidden)

    @pl.when(pl.program_id(0) == 0)
    def _():
        dup_ref[...] = dup
        ddown_ref[...] = ddown

    @pl.when(pl.program_id(0) > 0)
    def _():
        dup_ref[...] += dup
        ddown_ref[...] += ddown


def return_kernel(dims, ret_ref, cot_ref, hid_ref, moe_ref, gate_ref, gated_ref, y_ref, u_ref, z_ref, dt_ref,
                  proj_ref, vec_ref, out_ref, gain_ref, router_ref, route_ref, place_ref,
                  block_ref, ghid_ref, gy_ref, gz_ref, dout_ref, drouter_ref, dskip_ref, dgain_ref, adj_ref):
    seqs, rows, inner, states, rank, taps = dims
    count = seqs * rows
    total, width = ret_ref.shape[0], hid_ref.shape[1]
    pick = (lanes((count, total)) == place_ref[...]).astype(jnp.bfloat16)
    result = dot(pick, ret_ref[:, :width])
    hid, gate = hid_ref[...], gate_ref[...]
    block_ref[...] = (hid + gate * result).astype(jnp.bfloat16)
    cot = cot_ref[...].astype(jnp.float32)
    grad_gate = jnp.sum(cot * result, axis=1, keepdims=True)
    wide = (count, router_ref.shape[1])
    grad_logits = jnp.where(lanes(wide) == route_ref[...], grad_gate * gate * (1.0 - gate), 0.0).astype(jnp.bfloat16)
    grad_in = dot(pick, ret_ref[:, width:]) + dot_nt(grad_logits, router_ref[...])
    drouter_ref[...] = dot_tn(moe_ref[...], grad_logits)
    r2 = normalize(hid)
    dgain_ref[...] = jnp.sum(grad_in * (hid * r2), axis=0, keepdims=True)
    scaled = grad_in * gain_ref[1:2]
    grad_hid = cot + r2 * scaled - hid * (r2 * r2 * r2) * jnp.mean(scaled * hid, axis=1, keepdims=True)
    ghid_ref[...] = grad_hid
    branch = grad_hid.astype(jnp.bfloat16)
    for j in range(inner // WIDE):
        cols = slice(j * WIDE, (j + 1) * WIDE)
        dout_ref[cols, :] = dot_tn(gated_ref[:, cols], branch).astype(jnp.bfloat16)
        grad = dot_nt(branch, out_ref[cols, :])
        z = z_ref[:, cols]
        sig = sigmoid(z)
        gy = grad * (z * sig)
        gy_ref[:, cols] = gy
        gz_ref[:, cols] = (grad * y_ref[:, cols] * (sig + z * sig * (1.0 - sig))).astype(jnp.bfloat16)
        dskip_ref[:, cols] = jnp.sum(gy * u_ref[:, cols], axis=0, keepdims=True)
    a2 = -jnp.exp(vec_ref[0:states]) * LOG2E
    blocks = inner // 128
    for s in range(seqs):
        def eight(i, ms):
            ms = list(ms)
            at = pl.multiple_of((s + 1) * rows - 8 - i * 8, 8)
            small = proj_ref[pl.ds(at, 8), :]
            cs = [column(small[j : j + 1], rank + states, states) for j in range(8)]
            for k in range(blocks):
                sl = slice(k * 128, (k + 1) * 128)
                d8, g8 = dt_ref[pl.ds(at, 8), sl], gy_ref[pl.ds(at, 8), sl]
                for j in reversed(range(8)):
                    ms[k] = jnp.exp2(d8[j : j + 1] * a2[:, sl]) * (ms[k] + cs[j] * g8[j : j + 1])
            return tuple(ms)
        zero = jnp.zeros((states, 128), jnp.float32)
        ms = lax.fori_loop(0, rows // 8, eight, (zero,) * blocks)
        for k in range(blocks):
            adj_ref[s, :, k * 128 : (k + 1) * 128] = ms[k]


def back_kernel(dims, tok_ref, halo_ref, ext_ref, hist_ref, later_ref, gy_ref, gz_ref, ghid_ref, u_ref, dt_ref,
                proj_ref, win_ref, small_ref, vec_ref, gain_ref,
                dtok_ref, dhalo_ref, din_ref, dsmall_ref, dvec_ref, dgain_ref,
                hbuf, abuf, rbuf, ccol, adj, gdt, gu, gproj, gpad, gm, xn, gpre, sem):
    seqs, rows, inner, states, rank, taps = dims
    count = seqs * rows
    groups = rows // GROUP
    size = GROUP * states
    steps = seqs * groups

    def fetch(i, slot):
        s, g = i // groups, groups - 1 - i % groups
        at = pl.multiple_of(g * size, size)
        return pltpu.make_async_copy(hist_ref.at[s, pl.ds(at, size + states)], hbuf.at[slot], sem.at[slot])

    fetch(0, 0).start()
    dvec_ref[...] = jnp.zeros_like(dvec_ref)
    ones = (lanes((GROUP, size)) // states == subs((GROUP, size))).astype(jnp.bfloat16)

    def group(i, carry):
        slot = i % 2
        s, g = i // groups, groups - 1 - i % groups

        @pl.when(i + 1 < steps)
        def _():
            fetch(i + 1, 1 - slot).start()

        @pl.when(g == groups - 1)
        def _():
            adj[...] = later_ref[s]
        fetch(i, slot).wait()
        at = pl.multiple_of(s * rows + g * GROUP, GROUP)
        small = proj_ref[pl.ds(at, GROUP), :]
        bmix = block_diagonal(small, rank, states)
        for t in range(GROUP):
            cbuf_t = column(small[t : t + 1], rank + states, states)
            ccol[t] = cbuf_t

        def pair(c, carry2):
            gb, gc = carry2
            c0 = pl.multiple_of(c * WIDE, WIDE)
            for half in range(WIDE // 128):
                sl = pl.ds(pl.multiple_of(c0 + half * 128, 128), 128)
                hl = slice(half * 128, (half + 1) * 128)
                rates = -jnp.exp(vec_ref[0:states, sl])
                a2 = rates * LOG2E
                m = adj[:, sl]
                dd = dvec_ref[0:states, sl]
                for h8 in reversed(range(GROUP // 8)):
                    a8 = pl.multiple_of(at + h8 * 8, 8)
                    d8, g8 = dt_ref[pl.ds(a8, 8), sl], gy_ref[pl.ds(a8, 8), sl]
                    for j in reversed(range(8)):
                        t = h8 * 8 + j
                        a = m + ccol[t] * g8[j : j + 1]
                        m = jnp.exp2(d8[j : j + 1] * a2) * a
                        p = m * hbuf[slot, t * states : (t + 1) * states, sl].astype(jnp.float32) * rates
                        dd = dd + p * d8[j : j + 1]
                        abuf[t * states : (t + 1) * states, hl] = a.astype(jnp.bfloat16)
                        rbuf[t * states : (t + 1) * states, hl] = p.astype(jnp.bfloat16)
                adj[:, sl] = m
                dvec_ref[0:states, sl] = dd
            sl = pl.ds(c0, WIDE)
            d, g_, u = dt_ref[pl.ds(at, GROUP), sl], gy_ref[pl.ds(at, GROUP), sl], u_ref[pl.ds(at, GROUP), sl]
            w1, w2 = dot(ones, rbuf[...]), dot(bmix, abuf[...])
            gdt[pl.ds(at, GROUP), sl] = w1 + u * w2
            gu[pl.ds(at, GROUP), sl] = d * w2
            gb = gb + dot_nt((d * u).astype(jnp.bfloat16), abuf[...])
            gc = gc + dot_nt(g_.astype(jnp.bfloat16), hbuf[slot, states:, sl])
            return gb, gc
        zero = jnp.zeros((GROUP, size), jnp.float32)
        gb, gc = lax.fori_loop(0, inner // WIDE, pair, (zero, zero))
        place = (size, small.shape[1])
        own = subs(place) % states
        put = lambda base: (lanes(place) == own + base).astype(jnp.bfloat16)
        only = lambda v: jnp.where(ones > 0, v, 0.0).astype(jnp.bfloat16)
        gproj[pl.ds(at, GROUP), :] = dot(only(gb), put(rank)) + dot(only(gc), put(rank + states))
        return carry
    lax.fori_loop(0, steps, group, 0)

    low = rank_lanes(proj_ref[...], rank, states)
    at = rank + 2 * states
    row = states + taps
    grad_rank = jnp.zeros(proj_ref.shape, jnp.float32)
    for j in range(inner // WIDE):
        cols = slice(j * WIDE, (j + 1) * WIDE)
        pre = dot_nt(low, small_ref[cols, :]) + vec_ref[row + 1 : row + 2, cols]
        grad_pre = gdt[:, cols] * sigmoid(pre)
        dvec_ref[row + 1 : row + 2, cols] = jnp.sum(grad_pre, axis=0, keepdims=True)
        grad_pre = grad_pre.astype(jnp.bfloat16)
        gpre[:, cols] = grad_pre
        grad_rank = grad_rank + dot(grad_pre, small_ref[cols, :])
    where = lanes(grad_rank.shape)
    grad_rank = pltpu.roll(grad_rank, small_ref.shape[1] - at, axis=1)
    grad_proj = jnp.where(where < rank, grad_rank, jnp.where(where < at, gproj[...], 0.0)).astype(jnp.bfloat16)
    for ref, to in ((tok_ref, 0), (halo_ref, count)):
        x = ref[...].astype(jnp.float32)
        xn[to : to + x.shape[0]] = (x * normalize(x) * gain_ref[0:1]).astype(jnp.bfloat16)
    grad_normed = jnp.zeros((gm.shape[0], xn.shape[1]), jnp.float32)
    first = ext_ref.shape[1] - rows - taps + 1
    for j in range(inner // WIDE):
        cols = slice(j * WIDE, (j + 1) * WIDE)
        dsmall_ref[cols, :] = (
            dot_tn(u_ref[:, cols].astype(jnp.bfloat16), grad_proj) + dot_tn(gpre[:, cols], low)
        ).astype(jnp.bfloat16)
        grad_u = dot_nt(grad_proj, small_ref[cols, :]) + gy_ref[:, cols] * vec_ref[row + 2 : row + 3, cols] + gu[:, cols]
        taps_sum = [0.0] * taps
        bias_sum = 0.0
        heads = []
        for s in range(seqs):
            pre = conv_sum(ext_ref, s, cols, vec_ref, states, taps, rows)
            sig = sigmoid(pre)
            grad_conv = grad_u[s * rows : (s + 1) * rows] * (sig + pre * sig * (1.0 - sig))
            bias_sum = bias_sum + jnp.sum(grad_conv, axis=0, keepdims=True)
            for k in range(taps):
                taps_sum[k] = taps_sum[k] + jnp.sum(
                    grad_conv * ext_ref[s, first + k : first + k + rows, cols], axis=0, keepdims=True)
            gpad[0:8] = jnp.zeros((8, WIDE), jnp.float32)
            gpad[8 : 8 + rows] = grad_conv
            gpad[8 + rows :] = jnp.zeros((8, WIDE), jnp.float32)
            grad = 0.0
            for k in range(taps):
                grad = grad + vec_ref[states + k : states + k + 1, cols] * gpad[taps - 1 - k : taps + 7 - k + rows]
            heads.append(grad[0:8])
            gm[s * rows : (s + 1) * rows, cols] = grad[8:].astype(jnp.bfloat16)
        gm[count:, cols] = jnp.concatenate(heads).astype(jnp.bfloat16)
        dvec_ref[row : row + 1, cols] = bias_sum
        for k in range(taps):
            dvec_ref[states + k : states + k + 1, cols] = taps_sum[k]
        zcols = slice(inner + j * WIDE, inner + (j + 1) * WIDE)
        din_ref[:, cols] = dot_tn(xn[...], gm[:, cols]).astype(jnp.bfloat16)
        din_ref[:, zcols] = dot_tn(xn[:count], gz_ref[:, cols]).astype(jnp.bfloat16)
        gz = jnp.concatenate([gz_ref[:, cols], jnp.zeros((gm.shape[0] - count, WIDE), jnp.bfloat16)])
        grad_normed = grad_normed + dot_nt(gm[:, cols], win_ref[:, cols]) + dot_nt(gz, win_ref[:, zcols])
    gain_sum = 0.0
    for ref, to, base, out in ((tok_ref, 0, ghid_ref, dtok_ref), (halo_ref, count, None, dhalo_ref)):
        x = ref[...].astype(jnp.float32)
        r1 = normalize(x)
        grad = grad_normed[to : to + x.shape[0]]
        gain_sum = gain_sum + jnp.sum(grad * (x * r1), axis=0, keepdims=True)
        grad = grad * gain_ref[0:1]
        grad = r1 * grad - x * (r1 * r1 * r1) * jnp.mean(grad * x, axis=1, keepdims=True)
        out[...] = grad if base is None else grad + base[...]
    dgain_ref[...] = gain_sum


def like(*shape, dtype=f32):
    return jax.ShapeDtypeStruct(shape, dtype)


def params(mib=56):
    return pltpu.CompilerParams(vmem_limit_bytes=mib << 20)


def body(
    tokens,
    in_proj,
    conv_weight,
    conv_bias,
    state_proj,
    step_proj,
    step_bias,
    decay_log,
    skip_gain,
    out_proj,
    norm_gain,
    moe_gain,
    router_proj,
    expert_up,
    expert_down,
    routes,
    slot_index,
    cotangent,
):
    batch, seq = lax.axis_size("batch"), lax.axis_size("seq")
    both = ("batch", "seq")
    seqs, rows, width = tokens.shape
    count = seqs * rows
    devices = batch * seq
    taps, share = conv_weight.shape
    inner = share * devices
    states, rank = decay_log.shape[0], step_proj.shape[0]
    low_share = norm_gain.shape[0]
    experts = router_proj.shape[1]
    capacity = max(2, 5 * count // (4 * experts))
    dims = (seqs, rows, inner, states, rank, taps)
    tile = 128

    vectors = jnp.concatenate([decay_log, conv_weight, conv_bias[None], step_bias[None], skip_gain[None]])
    features = jnp.concatenate([router_proj, norm_gain[:, None], moe_gain[:, None]], axis=1)
    used = vectors.shape[0]
    room = -(-used // 8) * 8
    tail = jnp.concatenate(
        [
            state_proj,
            step_proj.T,
            jnp.pad(vectors, ((0, room - used), (0, 0))).T,
            jnp.pad(features, ((0, share - low_share), (0, tile - room - features.shape[1]))),
        ],
        axis=1,
    )
    halo = lax.ppermute(tokens[:, rows - taps + 1 :], "seq", [(i, i + 1) for i in range(seq - 1)])
    halo = jnp.pad(halo, ((0, 0), (8 - taps + 1, 0), (0, 0))).reshape(seqs * 8, width)
    if tuned(batch, seq):
        in_full, out_full, tail_full = gather_all(batch, seq, in_proj, out_proj, tail)
    else:
        in_full, out_full, tail_full = (
            lax.all_gather(a, both, axis=0, tiled=True) for a in (in_proj, out_proj, tail)
        )
    small = tail_full[:, :tile]
    vec = tail_full[:, tile : tile + room].T.astype(f32)
    model = tail_full[:, tile + room : tile + room + experts + 2]
    model = model.reshape(devices, share, experts + 2)[:, :low_share].reshape(width, experts + 2)
    gain = model[:, experts:].T.astype(f32)
    router = jnp.pad(model[:, :experts], ((0, 0), (0, tile - experts)))
    tok, cot = tokens.reshape(count, width), cotangent.reshape(count, width)
    route, slot = routes.reshape(count, 1), slot_index.reshape(count, 1)
    place = jnp.where(slot < capacity, route * capacity + slot, -1)

    ext, z, u, dt, proj, end, dsum = pl.pallas_call(
        partial(enter_kernel, dims),
        out_shape=[
            like(seqs, rows + 8, inner),
            like(count, inner),
            like(count, inner),
            like(count, inner),
            like(count, tile),
            like(seqs, states, inner),
            like(seqs, 1, inner),
        ],
        in_specs=[VM] * 6,
        out_specs=[VM] * 7,
        scratch_shapes=[pltpu.VMEM((count + seqs * 8, width), bf16)],
        compiler_params=params(),
        name="enter",
    )(tok, halo, in_full, small, vec, gain)
    rates = -jnp.exp(vec[:states])
    before = chain_states(seq, True, dsum, rates, end)
    size = GROUP * states
    total = experts * capacity
    hist, y, hid, gated, moe_in, gate, sent = pl.pallas_call(
        partial(leave_kernel, dims, capacity),
        out_shape=[
            like(seqs, (rows + 1) * states, inner, dtype=bf16),
            like(count, inner),
            like(count, width),
            like(count, inner, dtype=bf16),
            like(count, width, dtype=bf16),
            like(count, 1),
            like(total, 2 * width, dtype=bf16),
        ],
        in_specs=[VM] * 14,
        out_specs=[HBM] + [VM] * 6,
        scratch_shapes=[
            pltpu.VMEM((2, size, inner), bf16),
            pltpu.VMEM((seqs, states, inner), bf16),
            pltpu.SemaphoreType.DMA((2,)),
            pltpu.SemaphoreType.DMA((seqs,)),
        ],
        compiler_params=params(),
        name="leave",
    )(tok, cot, before, dt, u, z, proj, vec, out_full, gain, router, route, slot, place.reshape(1, count))

    spread = spread_rows(batch, seq, sent.reshape(experts, capacity, 2 * width))
    block = seq * capacity
    hidden_share = expert_up.shape[2]
    part, d_up, d_down = pl.pallas_call(
        expert_kernel,
        out_shape=[
            like(batch * block, 2 * width, dtype=bf16),
            like(width, hidden_share),
            like(hidden_share, width),
        ],
        grid=(batch,),
        in_specs=[
            pl.BlockSpec((block, 2 * width), lambda i: (i, 0)),
            pl.BlockSpec((width, hidden_share), lambda i: (0, 0)),
            pl.BlockSpec((hidden_share, width), lambda i: (0, 0)),
        ],
        out_specs=[
            pl.BlockSpec((block, 2 * width), lambda i: (i, 0)),
            pl.BlockSpec((width, hidden_share), lambda i: (0, 0)),
            pl.BlockSpec((hidden_share, width), lambda i: (0, 0)),
        ],
        compiler_params=params(),
        name="experts",
    )(spread.reshape(batch * block, 2 * width), expert_up[0], expert_down[0])
    back = collect_rows(batch, seq, part.reshape(batch, seq, capacity, 2 * width)).reshape(total, 2 * width)

    block_out, ghid, gy, gz, d_out, d_router, d_skip, d_moe, adj = pl.pallas_call(
        partial(return_kernel, dims),
        out_shape=[
            like(count, width, dtype=bf16),
            like(count, width),
            like(count, inner),
            like(count, inner, dtype=bf16),
            like(inner, width, dtype=bf16),
            like(width, tile),
            like(1, inner),
            like(1, width),
            like(seqs, states, inner),
        ],
        in_specs=[VM] * 17,
        out_specs=[VM] * 9,
        compiler_params=params(),
        name="back_experts",
    )(back, cot, hid, moe_in, gate, gated, y, u, z, dt, proj, vec, out_full, gain, router, route, place)
    later = chain_states(seq, False, dsum, rates, adj)
    d_tok, d_halo, d_in, d_small, d_vec, d_norm = pl.pallas_call(
        partial(back_kernel, dims),
        out_shape=[
            like(count, width),
            like(seqs * 8, width),
            like(width, 2 * inner, dtype=bf16),
            like(inner, tile, dtype=bf16),
            like(room, inner),
            like(1, width),
        ],
        in_specs=[VM] * 3 + [HBM] + [VM] * 11,
        out_specs=[VM] * 6,
        scratch_shapes=[
            pltpu.VMEM((2, size + states, inner), bf16),
            pltpu.VMEM((size, WIDE), bf16),
            pltpu.VMEM((size, WIDE), bf16),
            pltpu.VMEM((GROUP, states, tile), f32),
            pltpu.VMEM((states, inner), f32),
            pltpu.VMEM((count, inner), f32),
            pltpu.VMEM((count, inner), f32),
            pltpu.VMEM((count, tile), f32),
            pltpu.VMEM((rows + 16, WIDE), f32),
            pltpu.VMEM((count + seqs * 8, inner), bf16),
            pltpu.VMEM((count + seqs * 8, width), bf16),
            pltpu.VMEM((count, inner), bf16),
            pltpu.SemaphoreType.DMA((2,)),
        ],
        compiler_params=params(),
        name="back_mixer",
    )(tok, halo, ext, hist, later, gy, gz, ghid, u, dt, proj, in_full, small, vec, gain)

    d_model = jnp.concatenate([d_router[:, :experts], d_norm.T, d_moe.T], axis=1)
    d_model = jnp.pad(
        d_model.reshape(devices, low_share, experts + 2),
        ((0, 0), (0, share - low_share), (0, tile - room - experts - 2)),
    ).reshape(inner, tile - room)
    skip_row = states + taps + 2
    d_vec = d_vec.at[skip_row].set(d_skip[0])
    d_tail = jnp.concatenate([d_small, d_vec.T.astype(bf16), d_model.astype(bf16)], axis=1)
    if tuned(batch, seq):
        s_in, s_out, s_tail = reduce_all(batch, seq, d_in, d_out, d_tail)
    else:
        s_in, s_out, s_tail = (
            lax.psum_scatter(a.astype(f32), both, scatter_dimension=0, tiled=True) for a in (d_in, d_out, d_tail)
        )
    from_next = lax.ppermute(
        d_halo.reshape(seqs, 8, width)[:, 8 - taps + 1 :], "seq", [(i + 1, i) for i in range(seq - 1)]
    )
    d_tok = d_tok.reshape(tokens.shape).at[:, rows - taps + 1 :].add(from_next)
    s_vec = s_tail[:, tile : tile + room].T
    s_model = s_tail[:low_share, tile + room :]
    return (
        block_out.reshape(tokens.shape),
        d_tok,
        s_in,
        s_vec[states : states + taps],
        s_vec[states + taps],
        s_tail[:, : rank + 2 * states],
        s_tail[:, rank + 2 * states : tile].T,
        s_vec[states + taps + 1],
        s_vec[:states],
        s_vec[states + taps + 2],
        s_out,
        s_model[:, experts],
        s_model[:, experts + 1],
        s_model[:, :experts],
        d_up[None],
        d_down[None],
    )


def solution(mesh):
    in_specs = (
        P("batch", "seq", None),
        P(("batch", "seq"), None),
        P(None, ("batch", "seq")),
        P(("batch", "seq")),
        P(("batch", "seq"), None),
        P(None, ("batch", "seq")),
        P(("batch", "seq")),
        P(None, ("batch", "seq")),
        P(("batch", "seq")),
        P(("batch", "seq"), None),
        P(("batch", "seq")),
        P(("batch", "seq")),
        P(("batch", "seq"), None),
        P("seq", None, "batch"),
        P("seq", "batch", None),
        P("batch", "seq"),
        P("batch", "seq"),
        P("batch", "seq", None),
    )
    out_specs = (
        P("batch", "seq", None),
        P("batch", "seq", None),
        P(("batch", "seq"), None),
        P(None, ("batch", "seq")),
        P(("batch", "seq")),
        P(("batch", "seq"), None),
        P(None, ("batch", "seq")),
        P(("batch", "seq")),
        P(None, ("batch", "seq")),
        P(("batch", "seq")),
        P(("batch", "seq"), None),
        P(("batch", "seq")),
        P(("batch", "seq")),
        P(("batch", "seq"), None),
        P("seq", None, "batch"),
        P("seq", "batch", None),
    )
    return jax.shard_map(body, mesh=mesh, in_specs=in_specs, out_specs=out_specs, check_vma=False)
```

time: 2290 us -> 408 us (0.18); the launches traced: 2260 us -> 406 us
  waiting for transfers between devices: 670 us -> 1.2 us
  other arithmetic: 608 us -> 7.03 us
  blocking collectives: 529 us -> 0 us
  Pallas kernels: 0 us -> 361 us
  local copies, waits for them, and re-layouts: 312 us -> 29.6 us
  matrix products: 88.7 us -> 0 us
    reduce_scatter x5 -> x0, waiting for transfers between devices: 448 us -> none  [the longest x1 142 us: body(): lax.psum_scatter(grad_in_proj, ('batch', 'seq'), scatter_dimension=0, til...]
    all_gather x8 -> x0, blocking collectives: 433 us -> none  [the longest x2 67.9 us: prefix(): lax.all_gather(part.astype(kind), axis)]
    pallas_call x0 -> x11, Pallas kernels: none -> 361 us  [the longest x1 67.4 us: reduce_all(): pl.pallas_call(functools.partial(reduce_kernel, batch, seq, n), out_shape...]
    reduce_sum x392 -> x0, other arithmetic: 304 us -> none  [the longest x128 176 us: advance(): now_b[:, :, None] * (now_dt * now_u)[:, None, :]]
    unnamed x15 -> x0, waiting for transfers between devices: 198 us -> none
    dynamic_update_slice x384 -> x0, other arithmetic: 192 us -> none  [through_block(): return lax.scan(partial(advance, decay_rates), running, block)]
    mul x769 -> x0, local copies, waits for them, and re-layouts: 101 us -> none  [the longest x384 95.8 us: advance(): now_b[:, :, None] * (now_dt * now_u)[:, None, :]]
    dot_general x21 -> x0, matrix products: 88.7 us -> none  [the longest x1 13.4 us: body(): jnp.einsum('sxcf,sxcd->xfd', activated.astype(jnp.bfloat16), grouped_grad...]
  transfers between devices with their start and end apart: 17 -> 2, of which waited for: 10 -> 1; matrix products, arithmetic and copies ran while one was open for 10% -> 5% of each run, Pallas kernels for 0% -> 10%
where the time goes in v1:
time: 408 us; the launch traced here: 406 us
  Pallas kernels  361 us (88%)
  local copies, waits for them, and re-layouts  29.6 us (7%)
  other arithmetic  7.03 us (2%)
  starting transfers between devices  6.16 us (2%)
    pallas_call x1, Pallas kernels, reduce_all(): pl.pallas_call(functools.partial(reduce_kernel, batch, seq, n), out_shape...  67.4 us
    pallas_call x1, Pallas kernels, body(): pl.pallas_call(partial(back_kernel, dims), out_shape=[like(count, width),...  56 us
    pallas_call x1, Pallas kernels, spread_rows(): pl.pallas_call(functools.partial(spread_kernel, batch, seq), out_shape=ja...  55.4 us
    pallas_call x1, Pallas kernels, gather_all(): pl.pallas_call(functools.partial(gather_kernel, batch, seq, n), out_shape...  40.7 us
    pallas_call x1, Pallas kernels, collect_rows(): pl.pallas_call(functools.partial(collect_kernel, batch, seq), out_shape=j...  34.9 us
    pallas_call x2, Pallas kernels, chain_states(): pl.pallas_call(functools.partial(chain_kernel, seq, forward), out_shape=j...  34.5 us
    pallas_call x1, Pallas kernels, body(): pl.pallas_call(expert_kernel, out_shape=[like(batch * block, 2 * width, d...  21 us
    pallas_call x1, Pallas kernels, body(): pl.pallas_call(partial(leave_kernel, dims, capacity), out_shape=[like(seq...  19 us
  transfers between devices with their start and end apart: 2, of which 1 were waited for; matrix products, arithmetic and copies ran while one was open for 5% of the time, Pallas kernels for 10%

profile of v1, /device:TPU:0, one launch (start us, length us, event | category | flops | bytes accessed | tf_op | source)
XLA Modules:
  0.0 405.7 jit_solution(6319473882119822890)
XLA Ops:
  0.7 0.8 slice.107
  1.4 4.9 %collective-permute-start = (bf16[2,3,768]{2,1,0:T(4,128)(2,1)S(1)}, bf16[2,3,768]{2,1,0:T(4,128)(2,1)S(1)}, u32[]{:S(2)}, u32[]{:S(2)}) collective-permute-start(bf16[2,3,768]{2,1,0:T(4,128)(2,1)S(1)} %slice.107), channel_id=1, source_target_pairs={{0,1},{1,2},{2,3},{3,4},{4,5},{5,6},{6,7},{8,9},{9,10},{10,11},{11... | collective-permute-start | bytes 27656 | tf_op jit(solution)/shard_map/ppermute | solution.py:1063
  7.8 0.8 copy.115
  8.6 0.8 copy.111
  10.1 0.8 copy.109
  10.9 0.8 copy.113
  11.7 0.8 copy.110
  12.4 0.8 copy.114
  13.4 1.4 pad_maximum_fusion.2.refs_2_
  14.8 40.7 %gather_weights.1 = (bf16[768,3072]{1,0:T(8,128)(2,1)}, bf16[1536,768]{1,0:T(8,128)(2,1)}, bf16[1536,256]{1,0:T(8,128)(2,1)}) custom-call(bf16[24,3072]{1,0:T(8,128)(2,1)} %refs_0_.1, bf16[48,768]{1,0:T(8,128)(2,1)} %refs_1_.1, bf16[48,256]{1,0:T(8,128)(2,1)} %pad_maximum_fusion.2.refs_2_), custom_call_target="tpu_custom_call" | custom-call | tf_op jit(solution)/shard_map/gather_weights/pallas_call | solution.py:172
  55.5 1.2 slice.110
  56.7 1.5 copy.118
  60.6 0.8 slice.108.small_ref
  63.4 15.5 %enter.1 = (f32[2,136,1536]{2,1,0:T(8,128)}, f32[256,1536]{1,0:T(8,128)}, f32[256,1536]{1,0:T(8,128)}, f32[256,1536]{1,0:T(8,128)}, f32[256,128]{1,0:T(8,128)}, ...) custom-call(bf16[256,768]{1,0:T(8,128)(2,1)} %bitcast.45, bf16[16,768]{1,0:T(8,128)(2,1)} %pad_bitcast_fusion.halo_ref, ...), custom_call_target="tpu_custom_call" | custom-call | tf_op jit(solution)/shard_map/enter/pallas_call | solution.py:1081
  78.9 5.8 %chain_forward.1.h0_ref = f32[2,16,1536]{2,1,0:T(8,128)} custom-call(f32[2,1,1536]{2,1,0:T(1,128)} %get-tuple-element.80.dsum_ref, f32[16,1536]{1,0:T(8,128)} %fusion.rates_ref, f32[2,16,1536]{2,1,0:T(8,128)} %get-tuple-element.81.end_ref), custom_call_target="tpu_custom_call" | custom-call | tf_op jit(solution)/shard_map/chain_forward/pallas_call | solution.py:568
  84.8 19.0 %leave.1 = (bf16[2,2064,1536]{2,1,0:T(8,128)(2,1)}, f32[256,1536]{1,0:T(8,128)}, f32[256,768]{1,0:T(8,128)}, bf16[256,1536]{1,0:T(8,128)(2,1)}, bf16[256,768]{1,...) custom-call(bf16[256,768]{1,0:T(8,128)(2,1)} %bitcast.46, bf16[256,768]{1,0:T(8,128)(2,1)} %bitcast.50, ...), custom_call_target="tpu_custom_call" | custom-call | tf_op jit(solution)/shard_map/leave/pallas_call | solution.py:1102
  103.7 55.4 %spread_rows.1 = bf16[4,8,40,1536]{3,2,1,0:T(8,128)(2,1)} custom-call(bf16[8,40,1536]{2,1,0:T(8,128)(2,1)} %bitcast.56), custom_call_target="tpu_custom_call" | custom-call | tf_op jit(solution)/shard_map/spread_rows/pallas_call | solution.py:411
  159.1 21.0 %experts.1 = (bf16[1280,1536]{1,0:T(8,128)(2,1)}, f32[768,768]{1,0:T(8,128)}, f32[768,768]{1,0:T(8,128)}) custom-call(bf16[1280,1536]{1,0:T(8,128)(2,1)} %bitcast.44, bf16[768,768]{1,0:T(8,128)(2,1)} %bitcast.54, bf16[768,768]{1,0:T(8,128)(2,1)} %bitcast.55), custom_call_target="tpu_custom_call" | custom-call | tf_op jit(solution)/shard_map/experts/pallas_call | solution.py:1128
  180.0 2.1 copy-done.2
  182.2 34.9 %collect_rows.1 = bf16[8,40,1536]{2,1,0:T(8,128)(2,1)S(1)} custom-call(bf16[4,8,40,1536]{3,2,1,0:T(8,128)(2,1)S(1)} %bitcast.43), custom_call_target="tpu_custom_call" | custom-call | tf_op jit(solution)/shard_map/collect_rows/pallas_call | solution.py:501
  217.1 0.9 copy-done.1
  218.0 16.4 %back_experts.1 = (bf16[256,768]{1,0:T(8,128)(2,1)}, f32[256,768]{1,0:T(8,128)}, f32[256,1536]{1,0:T(8,128)}, bf16[256,1536]{1,0:T(8,128)(2,1)}, bf16[1536,768]{...) custom-call(bf16[320,1536]{1,0:T(8,128)(2,1)} %bitcast.42, ...), custom_call_target="tpu_custom_call" | custom-call | tf_op jit(solution)/shard_map/back_experts/pallas_call | solution.py:1151
  235.3 28.7 %chain_backward.1.later_ref = f32[2,16,1536]{2,1,0:T(8,128)} custom-call(f32[2,1,1536]{2,1,0:T(1,128)} %get-tuple-element.80.dsum_ref, f32[16,1536]{1,0:T(8,128)} %fusion.rates_ref, f32[2,16,1536]{2,1,0:T(8,128)} %get-tuple-element.97.end_ref), custom_call_target="tpu_custom_call" | custom-call | tf_op jit(solution)/shard_map/chain_backward/pallas_call | solution.py:568
  264.0 56.0 %back_mixer.1 = (f32[256,768]{1,0:T(8,128)}, f32[16,768]{1,0:T(8,128)}, bf16[768,3072]{1,0:T(8,128)(2,1)}, bf16[1536,128]{1,0:T(8,128)(2,1)}, f32[24,1536]{1,0:T(8,128)}, /*index=5*/f32[1,768]{1,0:T(1,128)}) custom-call(bf16[256,768]{1,0:T(8,128)(2,1)} %bitcast.47, bf16[16,768]{1,0:T(8,128)(2,1)} %pad_bitcast_fusion.halo_ref, ...), custom_call_target="tpu_custom_call" | custom-call | tf_op jit(solution)/shard_map/back_mixer/pallas_call | solution.py:1170
  322.1 1.5 scatter.4
  323.5 1.2 pad_maximum_fusion.refs_2_
  324.8 2.3 copy-done
  327.1 67.4 %reduce_grads.1 = (f32[24,3072]{1,0:T(8,128)S(1)}, f32[48,768]{1,0:T(8,128)S(1)}, f32[48,256]{1,0:T(8,128)S(1)}) custom-call(bf16[768,3072]{1,0:T(8,128)(2,1)S(1)} %copy-done, bf16[1536,768]{1,0:T(8,128)(2,1)S(1)} %copy-done.3, bf16[1536,256]{1,0:T(8,128)(2,1)S(1)} %pad_maximum_fusion.refs_2_), custom_call_target="tpu_custom_call" | custom-call | tf_op jit(solution)/shard_map/reduce_grads/pallas_call | solution.py:348
  394.7 1.3 collective-permute-start.1
  400.8 1.2 collective-permute-done.1
  402.0 0.8 slice_add_fusion
  402.8 1.5 scatter-add.4
  (70 shorter events, 16.1 us)
Async XLA Ops:
  0.6 57.5 %copy-start.12 = (s32[2,128]{1,0:T(2,128)S(1)}, s32[2,128]{1,0:T(2,128)}, u32[]{:S(2)}) copy-start(s32[2,128]{1,0:T(2,128)} %param.37) | copy-start | bytes 3076
  0.7 57.6 %copy-start.13 = (s32[2,128]{1,0:T(2,128)S(1)}, s32[2,128]{1,0:T(2,128)}, u32[]{:S(2)}) copy-start(s32[2,128]{1,0:T(2,128)} %param.38) | copy-start | bytes 3076
  1.4 61.4 %collective-permute-start = (bf16[2,3,768]{2,1,0:T(4,128)(2,1)S(1)}, bf16[2,3,768]{2,1,0:T(4,128)(2,1)S(1)}, u32[]{:S(2)}, u32[]{:S(2)}) collective-permute-start(bf16[2,3,768]{2,1,0:T(4,128)(2,1)S(1)} %slice.107), channel_id=1, source_target_pairs={{0,1},{1,2},{2,3},{3,4},{4,5},{5,6},{6,7},{8,9},{9,10},{10,11},{11... | collective-permute-start | bytes 27656 | tf_op jit(solution)/shard_map/ppermute | solution.py:1063
  56.6 3.9 copy-start.5
  58.3 4.5 %copy-start.6 = (s32[256,1]{1,0:T(8,128)}, s32[256,1]{1,0:T(8,128)S(1)}, u32[]{:S(2)}) copy-start(s32[256,1]{1,0:T(8,128)S(1)} %copy.121.route_ref) | copy-start | bytes 3076
  58.4 4.4 %copy-start.7 = (s32[256,1]{1,0:T(8,128)}, s32[256,1]{1,0:T(8,128)S(1)}, u32[]{:S(2)}) copy-start(s32[256,1]{1,0:T(8,128)S(1)} %copy.122.slot_ref) | copy-start | bytes 3076
  58.5 4.3 %copy-start.4 = (f32[24,1536]{1,0:T(8,128)}, f32[24,1536]{1,0:T(8,128)S(1)}, u32[]{:S(2)}) copy-start(f32[24,1536]{1,0:T(8,128)S(1)} %convert_bitcast_fusion.1.vec_ref) | copy-start | bytes 442372
  180.0 2.1 copy-start.2
  217.0 0.9 copy-start.1
  264.0 57.0 %copy-start.9 = (f32[768,128]{1,0:T(8,128)S(1)}, f32[768,128]{1,0:T(8,128)}, u32[]{:S(2)}) copy-start(f32[768,128]{1,0:T(8,128)} %get-tuple-element.108) | copy-start | bytes 1179652
  320.0 1.5 copy-start.8
  320.0 1.8 copy-start.11
  321.8 3.0 copy-start.3
  324.8 2.3 copy-start
  327.1 67.5 %copy-start.10 = (f32[16,768]{1,0:T(8,128)S(1)}, f32[16,768]{1,0:T(8,128)}, u32[]{:S(2)}) copy-start(f32[16,768]{1,0:T(8,128)} %get-tuple-element.102) | copy-start | bytes 147460
  394.7 7.4 %collective-permute-start.1 = (f32[2,3,768]{2,1,0:T(4,128)S(1)}, f32[2,3,768]{2,1,0:T(4,128)S(1)}, u32[]{:S(2)}, u32[]{:S(2)}) collective-permute-start(f32[2,3,768]{2,1,0:T(4,128)S(1)} %slice.135), channel_id=1, source_target_pairs={{1,0},{2,1},{3,2},{4,3},{5,4},{6,5},{7,6},{9,8},{10,9},{11,10},{12... | collective-permute-start | bytes 55304 | tf_op jit(solution)/shard_map/ppermute | solution.py:1215

commit v2 on v1

--- a/solution.py
+++ b/solution.py
@@ -357,168 +357,8 @@
     )(*sums)
 
 
-def spread_kernel(batch, seq, rows_ref, out_ref, local_sem, send_sem, recv_sem):
-    me = Place(batch, seq)
-    b, s = me.at()
-    sib, nx = me.at(c=1 - me.c), me.at(x=1 - me.x)
-    greet([(None, sib), (None, nx)] + [(None, (b, (s + k) % seq)) for k in range(1, seq)])
-    sends = []
-
-    def send(src, dst, recv, dev):
-        cp = pltpu.make_async_remote_copy(
-            src_ref=src, dst_ref=dst, send_sem=send_sem.at[len(sends)], recv_sem=recv,
-            device_id=dev, device_id_type=MESH)
-        cp.start()
-        sends.append(cp)
-
-    def arrived(bb, ss):
-        pltpu.make_async_remote_copy(
-            src_ref=out_ref.at[bb, ss], dst_ref=out_ref.at[bb, ss], send_sem=send_sem.at[0],
-            recv_sem=recv_sem.at[bb, ss], device_id=sib, device_id_type=MESH).wait_recv()
-
-    for k in range(seq - 1, 0, -1):
-        there = (s + k) % seq
-        send(rows_ref.at[there], out_ref.at[b, s], recv_sem.at[b, s], (b, there))
-    for dev in (nx, sib):
-        send(rows_ref.at[s], out_ref.at[b, s], recv_sem.at[b, s], dev)
-    local = pltpu.make_async_copy(rows_ref.at[s], out_ref.at[b, s], local_sem)
-    local.start()
-    near = nx[0]
-    for k in range(1, seq):
-        there = (s + k) % seq
-        arrived(b, there)
-        for dev in (nx, sib):
-            send(out_ref.at[b, there], out_ref.at[b, there], recv_sem.at[b, there], dev)
-        there = (s + k - 1) % seq
-        arrived(near, there)
-        send(out_ref.at[near, there], out_ref.at[near, there], recv_sem.at[near, there], sib)
-    there = (s + seq - 1) % seq
-    arrived(near, there)
-    send(out_ref.at[near, there], out_ref.at[near, there], recv_sem.at[near, there], sib)
-    for k in range(seq):
-        there = (s + k) % seq
-        arrived(sib[0], there)
-        arrived((1 - me.x) * 2 + 1 - me.c, there)
-    local.wait()
-    for cp in sends:
-        cp.wait_send()
-
-
-def spread_rows(batch, seq, rows):
-    if not tuned(batch, seq):
-        mine = lax.all_to_all(rows, "seq", split_axis=0, concat_axis=0, tiled=True)
-        return lax.all_gather(mine, "batch", axis=0)
-    return pl.pallas_call(
-        functools.partial(spread_kernel, batch, seq),
-        out_shape=jax.ShapeDtypeStruct((batch,) + rows.shape, rows.dtype),
-        in_specs=[HBM],
-        out_specs=HBM,
-        scratch_shapes=[
-            pltpu.SemaphoreType.DMA,
-            pltpu.SemaphoreType.DMA((seq - 1 + 2 * seq + seq,)),
-            pltpu.SemaphoreType.DMA((batch, seq)),
-        ],
-        compiler_params=pltpu.CompilerParams(collective_id=2, has_side_effects=True),
-        name="spread_rows",
-    )(rows)
-
-
 def tuned(batch, seq):
     return batch == 4 and seq == 8
-
-
-def collect_kernel(batch, seq, part_ref, out_ref, held, total, sib_buf, near_buf,
-                   load_sem, send_sem, sib_sem, near_sem, out_sem, local_sem):
-    me = Place(batch, seq)
-    b, s = me.at()
-    sib, nx = me.at(c=1 - me.c), me.at(x=1 - me.x)
-    greet([(None, sib), (None, nx)] + [(None, (b, (s + k) % seq)) for k in range(1, seq)])
-    sends = []
-
-    def send(src, dst, recv, dev):
-        cp = pltpu.make_async_remote_copy(
-            src_ref=src, dst_ref=dst, send_sem=send_sem.at[len(sends)], recv_sem=recv,
-            device_id=dev, device_id_type=MESH)
-        cp.start()
-        sends.append(cp)
-
-    def arrived(ref, recv):
-        pltpu.make_async_remote_copy(
-            src_ref=ref, dst_ref=ref, send_sem=send_sem.at[0],
-            recv_sem=recv, device_id=sib, device_id_type=MESH).wait_recv()
-
-    f32 = lambda ref: ref[...].astype(jnp.float32)
-    far_x = 1 - me.x
-    turn = lambda k: (s + 1 + k) % seq
-    loads = []
-    for k in range(seq):
-        t = turn(k)
-        for g, xx in enumerate((far_x, me.x)):
-            send(part_ref.at[xx * 2 + 1 - me.c, t], sib_buf.at[g, t], sib_sem.at[g, t], sib)
-            cp = pltpu.make_async_copy(part_ref.at[xx * 2 + me.c, t], held.at[g, t], load_sem.at[g, t])
-            cp.start()
-            loads.append(cp)
-
-    def first(k):
-        t = turn(k)
-        loads[2 * k].wait()
-        arrived(sib_buf.at[0, t], sib_sem.at[0, t])
-        total[0, t] = (f32(held.at[0, t]) + f32(sib_buf.at[0, t])).astype(jnp.bfloat16)
-        send(total.at[0, t], near_buf.at[t], near_sem.at[t], nx)
-
-    def second(k):
-        t = turn(k)
-        loads[2 * k + 1].wait()
-        arrived(sib_buf.at[1, t], sib_sem.at[1, t])
-        arrived(near_buf.at[t], near_sem.at[t])
-        total[1, t] = (f32(held.at[1, t]) + f32(sib_buf.at[1, t]) + f32(near_buf.at[t])).astype(jnp.bfloat16)
-        if k < seq - 1:
-            send(total.at[1, t], out_ref.at[s], out_sem.at[s], (b, t))
-        else:
-            cp = pltpu.make_async_copy(total.at[1, t], out_ref.at[s], local_sem)
-            cp.start()
-            return cp
-
-    first(0)
-    first(1)
-    for k in range(seq):
-        if k + 2 < seq:
-            first(k + 2)
-        own = second(k)
-    for k in range(1, seq):
-        t = (s + k) % seq
-        arrived(out_ref.at[t], out_sem.at[t])
-    own.wait()
-    for cp in sends:
-        cp.wait_send()
-
-
-def collect_rows(batch, seq, part):
-    if not tuned(batch, seq):
-        mine = lax.psum_scatter(part, "batch", scatter_dimension=0, tiled=False)
-        return lax.all_to_all(mine, "seq", split_axis=0, concat_axis=0, tiled=True)
-    slab = part.shape[2:]
-    return pl.pallas_call(
-        functools.partial(collect_kernel, batch, seq),
-        out_shape=jax.ShapeDtypeStruct((seq,) + slab, part.dtype),
-        in_specs=[HBM],
-        out_specs=HBM,
-        scratch_shapes=[
-            pltpu.VMEM((2, seq) + slab, part.dtype),
-            pltpu.VMEM((2, seq) + slab, part.dtype),
-            pltpu.VMEM((2, seq) + slab, part.dtype),
-            pltpu.VMEM((seq,) + slab, part.dtype),
-            pltpu.SemaphoreType.DMA((2, seq)),
-            pltpu.SemaphoreType.DMA((4 * seq - 1,)),
-            pltpu.SemaphoreType.DMA((2, seq)),
-            pltpu.SemaphoreType.DMA((seq,)),
-            pltpu.SemaphoreType.DMA((seq,)),
-            pltpu.SemaphoreType.DMA,
-        ],
-        compiler_params=pltpu.CompilerParams(
-            collective_id=3, has_side_effects=True, vmem_limit_bytes=32 << 20),
-        name="collect_rows",
-    )(part)
 
 
 def chain_kernel(seq, forward, dsum_ref, rates_ref, end_ref, out_ref, held, outgoing, send_sem, recv_sem):
@@ -582,6 +422,102 @@
     )(dsum, rates, end)
 
 
+def relay_kernel(seq, forward, states, dsum_ref, vec_ref, end_ref, out_ref, mine, theirs, their_sum, held, outgoing,
+                 pair_send, pair_recv, line_send, line_recv):
+    me = Place(4, seq)
+    y, z, last = me.y, me.z, me.Z - 1
+    step = 1 if forward else -1
+    first = y == (0 if forward else 1)
+    has_before = z > 0 if forward else z < last
+    has_after = z < last if forward else z > 0
+    pair, before, after = me.at(y=1 - y), me.at(z=z - step), me.at(z=z + step)
+    greet([(None, pair), (has_before, before), (has_after, after)])
+    count = end_ref.shape[0]
+    rates = -jnp.exp(vec_ref[0:states])
+
+    def swaps(i):
+        return [
+            pltpu.make_async_remote_copy(
+                src_ref=src, dst_ref=dst, send_sem=pair_send.at[i, k], recv_sem=pair_recv.at[i, k],
+                device_id=pair, device_id_type=MESH)
+            for k, (src, dst) in enumerate(((mine.at[i], theirs.at[i]), (dsum_ref.at[i], their_sum.at[i])))
+        ]
+
+    def onward(i):
+        return pltpu.make_async_remote_copy(
+            src_ref=outgoing.at[i], dst_ref=held.at[i], send_sem=line_send.at[i],
+            recv_sem=line_recv.at[i], device_id=after, device_id_type=MESH)
+
+    for i in range(count):
+        mine[i] = end_ref[i].astype(bf16)
+        for cp in swaps(i):
+            cp.start()
+    for i in range(count):
+        for cp in swaps(i):
+            cp.wait_recv()
+        own, other = end_ref[i], theirs[i].astype(f32)
+        own_sum, other_sum = dsum_ref[i], their_sum[i]
+        early, late = jnp.where(first, own, other), jnp.where(first, other, own)
+        early_sum, late_sum = jnp.where(first, own_sum, other_sum), jnp.where(first, other_sum, own_sum)
+        both = late + jnp.exp(rates * late_sum) * early
+
+        @pl.when(has_before)
+        def _():
+            onward(i).wait_recv()
+            arrived = held[i].astype(f32)
+            outgoing[i] = (both + jnp.exp(rates * (early_sum + late_sum)) * arrived).astype(bf16)
+
+        @pl.when(jnp.logical_not(has_before))
+        def _():
+            outgoing[i] = both.astype(bf16)
+
+        @pl.when(has_after)
+        def _():
+            onward(i).start()
+
+        @pl.when(has_before)
+        def _():
+            arrived = held[i].astype(f32)
+            out_ref[i] = jnp.where(first, arrived, early + jnp.exp(rates * early_sum) * arrived)
+
+        @pl.when(jnp.logical_not(has_before))
+        def _():
+            out_ref[i] = jnp.where(first, jnp.zeros_like(early), early)
+    for i in range(count):
+        for cp in swaps(i):
+            cp.wait_send()
+
+        @pl.when(has_after)
+        def _():
+            onward(i).wait_send()
+
+
+def relay_states(batch, seq, forward, states, dsum, vec, end):
+    if not tuned(batch, seq):
+        return chain_states(seq, forward, dsum, -jnp.exp(vec[:states]), end)
+    n = end.shape[0]
+    return pl.pallas_call(
+        functools.partial(relay_kernel, seq, forward, states),
+        out_shape=jax.ShapeDtypeStruct(end.shape, f32),
+        in_specs=[VM] * 3,
+        out_specs=VM,
+        scratch_shapes=[
+            pltpu.VMEM(end.shape, bf16),
+            pltpu.VMEM(end.shape, bf16),
+            pltpu.VMEM(dsum.shape, f32),
+            pltpu.VMEM(end.shape, bf16),
+            pltpu.VMEM(end.shape, bf16),
+            pltpu.SemaphoreType.DMA((n, 2)),
+            pltpu.SemaphoreType.DMA((n, 2)),
+            pltpu.SemaphoreType.DMA((n,)),
+            pltpu.SemaphoreType.DMA((n,)),
+        ],
+        compiler_params=pltpu.CompilerParams(
+            collective_id=6 if forward else 7, has_side_effects=True),
+        name="relay_forward" if forward else "relay_backward",
+    )(dsum, vec, end)
+
+
 def dot(a, b):
     return jnp.dot(a, b, preferred_element_type=jnp.float32)
 
@@ -612,13 +548,20 @@
     return jnp.broadcast_to(jnp.sum(only, axis=1, keepdims=True), shape)
 
 
-def block_diagonal(rows, base, states):
-    t = rows.shape[0]
-    pick = (rows.shape[1], t * states)
-    spread = (subs(pick) == lanes(pick) % states + base).astype(jnp.bfloat16)
-    wide = dot(rows.astype(jnp.bfloat16), spread)
-    own = lanes(wide.shape) // states == subs(wide.shape)
-    return jnp.where(own, wide, 0.0).astype(jnp.bfloat16)
+def row_sums(parts):
+    row = subs(parts[0].shape)
+    four, two, one = row < 4, (row // 2) % 2 == 0, row % 2 == 0
+    turn = lambda v, by: pltpu.roll(v, by, axis=0)
+    a = [
+        jnp.where(four, parts[j], parts[j + 4]) + turn(jnp.where(four, parts[j + 4], parts[j]), 4)
+        for j in range(4)
+    ]
+    b = [jnp.where(two, a[j] + turn(a[j], 6), a[j + 2] + turn(a[j + 2], 2)) for j in range(2)]
+    return jnp.where(one, b[0] + turn(b[0], 7), b[1] + turn(b[1], 1))
+
+
+def fold(v):
+    return sum(v[i : i + 8] for i in range(8, v.shape[0], 8)) + v[:8]
 
 
 WIDE = 256
@@ -725,17 +668,18 @@
                 at = pl.multiple_of(s * rows + g * GROUP + half * 8, 8)
                 small = proj_ref[pl.ds(at, 8), :]
                 bs = [column(small[j : j + 1], rank, states) for j in range(8)]
+                cs = [column(small[j : j + 1], rank + states, states) for j in range(8)]
                 for k in range(blocks):
                     sl = slice(k * 128, (k + 1) * 128)
                     d8 = dt_ref[pl.ds(at, 8), sl]
                     w8 = d8 * u_ref[pl.ds(at, 8), sl]
+                    parts = []
                     for j in range(8):
                         t = half * 8 + j
                         hs[k] = jnp.exp2(d8[j : j + 1] * a2[:, sl]) * hs[k] + bs[j] * w8[j : j + 1]
                         hbuf[slot, t * states : (t + 1) * states, sl] = hs[k].astype(jnp.bfloat16)
-            at = pl.multiple_of(s * rows + g * GROUP, GROUP)
-            mix = block_diagonal(proj_ref[pl.ds(at, GROUP), :], rank + states, states)
-            y_ref[pl.ds(at, GROUP), :] = dot(mix, hbuf[slot])
+                        parts.append(fold(cs[j] * hs[k]))
+                    y_ref[pl.ds(at, 8), sl] = row_sums(parts)
             out_copy(s, g, slot).start()
             return tuple(hs)
         hs = tuple(h0_ref[s, :, k * 128 : (k + 1) * 128] for k in range(blocks))
@@ -863,7 +807,7 @@
 def back_kernel(dims, tok_ref, halo_ref, ext_ref, hist_ref, later_ref, gy_ref, gz_ref, ghid_ref, u_ref, dt_ref,
                 proj_ref, win_ref, small_ref, vec_ref, gain_ref,
                 dtok_ref, dhalo_ref, din_ref, dsmall_ref, dvec_ref, dgain_ref,
-                hbuf, abuf, rbuf, ccol, adj, gdt, gu, gproj, gpad, gm, xn, gpre, sem):
+                hbuf, ccol, bcol, gbsum, gcsum, adj, gdt, gu, gproj, gpad, gm, xn, gpre, sem):
     seqs, rows, inner, states, rank, taps = dims
     count = seqs * rows
     groups = rows // GROUP
@@ -877,7 +821,7 @@
 
     fetch(0, 0).start()
     dvec_ref[...] = jnp.zeros_like(dvec_ref)
-    ones = (lanes((GROUP, size)) // states == subs((GROUP, size))).astype(jnp.bfloat16)
+    strip = 512
 
     def group(i, carry):
         slot = i % 2
@@ -890,52 +834,57 @@
         @pl.when(g == groups - 1)
         def _():
             adj[...] = later_ref[s]
-        fetch(i, slot).wait()
         at = pl.multiple_of(s * rows + g * GROUP, GROUP)
         small = proj_ref[pl.ds(at, GROUP), :]
-        bmix = block_diagonal(small, rank, states)
         for t in range(GROUP):
-            cbuf_t = column(small[t : t + 1], rank + states, states)
-            ccol[t] = cbuf_t
-
-        def pair(c, carry2):
-            gb, gc = carry2
-            c0 = pl.multiple_of(c * WIDE, WIDE)
-            for half in range(WIDE // 128):
-                sl = pl.ds(pl.multiple_of(c0 + half * 128, 128), 128)
-                hl = slice(half * 128, (half + 1) * 128)
-                rates = -jnp.exp(vec_ref[0:states, sl])
-                a2 = rates * LOG2E
-                m = adj[:, sl]
-                dd = dvec_ref[0:states, sl]
-                for h8 in reversed(range(GROUP // 8)):
-                    a8 = pl.multiple_of(at + h8 * 8, 8)
-                    d8, g8 = dt_ref[pl.ds(a8, 8), sl], gy_ref[pl.ds(a8, 8), sl]
-                    for j in reversed(range(8)):
-                        t = h8 * 8 + j
-                        a = m + ccol[t] * g8[j : j + 1]
-                        m = jnp.exp2(d8[j : j + 1] * a2) * a
-                        p = m * hbuf[slot, t * states : (t + 1) * states, sl].astype(jnp.float32) * rates
-                        dd = dd + p * d8[j : j + 1]
-                        abuf[t * states : (t + 1) * states, hl] = a.astype(jnp.bfloat16)
-                        rbuf[t * states : (t + 1) * states, hl] = p.astype(jnp.bfloat16)
-                adj[:, sl] = m
-                dvec_ref[0:states, sl] = dd
-            sl = pl.ds(c0, WIDE)
-            d, g_, u = dt_ref[pl.ds(at, GROUP), sl], gy_ref[pl.ds(at, GROUP), sl], u_ref[pl.ds(at, GROUP), sl]
-            w1, w2 = dot(ones, rbuf[...]), dot(bmix, abuf[...])
-            gdt[pl.ds(at, GROUP), sl] = w1 + u * w2
-            gu[pl.ds(at, GROUP), sl] = d * w2
-            gb = gb + dot_nt((d * u).astype(jnp.bfloat16), abuf[...])
-            gc = gc + dot_nt(g_.astype(jnp.bfloat16), hbuf[slot, states:, sl])
-            return gb, gc
-        zero = jnp.zeros((GROUP, size), jnp.float32)
-        gb, gc = lax.fori_loop(0, inner // WIDE, pair, (zero, zero))
-        place = (size, small.shape[1])
-        own = subs(place) % states
-        put = lambda base: (lanes(place) == own + base).astype(jnp.bfloat16)
-        only = lambda v: jnp.where(ones > 0, v, 0.0).astype(jnp.bfloat16)
-        gproj[pl.ds(at, GROUP), :] = dot(only(gb), put(rank)) + dot(only(gc), put(rank + states))
+            ccol[t] = column(small[t : t + 1], rank + states, states)
+            bcol[t] = column(small[t : t + 1], rank, states)
+            gbsum[t] = jnp.zeros((states, 128), f32)
+            gcsum[t] = jnp.zeros((states, 128), f32)
+        fetch(i, slot).wait()
+        for c0 in range(0, inner, strip):
+            sls = [slice(c0 + k, c0 + k + 128) for k in range(0, strip, 128)]
+            rates = [-jnp.exp(vec_ref[0:states, sl]) for sl in sls]
+            m = [adj[:, sl] for sl in sls]
+            dd = [dvec_ref[0:states, sl] for sl in sls]
+            for half in reversed(range(GROUP // 8)):
+                a8 = pl.multiple_of(at + half * 8, 8)
+                d8 = [dt_ref[pl.ds(a8, 8), sl] for sl in sls]
+                g8 = [gy_ref[pl.ds(a8, 8), sl] for sl in sls]
+                u8 = [u_ref[pl.ds(a8, 8), sl] for sl in sls]
+                w8 = [d * u for d, u in zip(d8, u8)]
+                r1, r2 = [[None] * 8 for _ in sls], [[None] * 8 for _ in sls]
+                for j in reversed(range(8)):
+                    t = half * 8 + j
+                    gb = gc = 0.0
+                    for k, sl in enumerate(sls):
+                        d, gy = d8[k][j : j + 1], g8[k][j : j + 1]
+                        a = m[k] + ccol[t] * gy
+                        m[k] = jnp.exp2(d * (rates[k] * LOG2E)) * a
+                        p = m[k] * hbuf[slot, t * states : (t + 1) * states, sl].astype(f32) * rates[k]
+                        dd[k] = dd[k] + p * d
+                        gb = gb + a * w8[k][j : j + 1]
+                        gc = gc + gy * hbuf[slot, (t + 1) * states : (t + 2) * states, sl].astype(f32)
+                        r1[k][j], r2[k][j] = fold(p), fold(a * bcol[t])
+                    gbsum[t] += gb
+                    gcsum[t] += gc
+                for k, sl in enumerate(sls):
+                    w1, w2 = row_sums(r1[k]), row_sums(r2[k])
+                    gdt[pl.ds(a8, 8), sl] = w1 + u8[k] * w2
+                    gu[pl.ds(a8, 8), sl] = d8[k] * w2
+            for k, sl in enumerate(sls):
+                adj[:, sl] = m[k]
+                dvec_ref[0:states, sl] = dd[k]
+        square = (states, small.shape[1])
+        where, entry = lanes(square), subs(square)
+        line = subs((GROUP, small.shape[1]))
+        out = jnp.zeros(small.shape, f32)
+        for t in range(GROUP):
+            gb = jnp.broadcast_to(jnp.sum(gbsum[t], axis=1, keepdims=True), square)
+            gc = jnp.broadcast_to(jnp.sum(gcsum[t], axis=1, keepdims=True), square)
+            put = jnp.where(where == entry + rank, gb, jnp.where(where == entry + rank + states, gc, 0.0))
+            out = jnp.where(line == t, jnp.sum(put, axis=0, keepdims=True), out)
+        gproj[pl.ds(at, GROUP), :] = out
         return carry
     lax.fori_loop(0, steps, group, 0)
 
@@ -1013,6 +962,289 @@
     return pltpu.CompilerParams(vmem_limit_bytes=mib << 20)
 
 
+def moe_kernel(seq, rows_ref, up_ref, down_ref, back_ref, land_ref, dup_ref, ddown_ref,
+               xbuf, part, act, ghid, hid, gact, sib_buf, near_buf, far_sum, own_sum,
+               local_sem, disp_sem, pass_sem, recv_sem, load_sem, sib_send, sib_recv, near_send, near_recv,
+               final_send, final_recv, final_local):
+    me = Place(4, seq)
+    b, s = me.at()
+    y, z, Z = me.y, me.z, me.Z
+    cap, wide = rows_ref.shape[1], rows_ref.shape[2]
+    width = wide // 2
+    two = 2 * cap
+    block = 4 * two
+    sib, nx = me.at(c=1 - me.c), me.at(x=1 - me.x)
+    near, beside, across = nx[0], sib[0], (1 - me.x) * 2 + 1 - me.c
+    greet([(None, sib), (None, nx)] + [(None, (b, (s + k) % seq)) for k in range(1, seq)])
+
+    def remote(src, dst, send, recv, dev):
+        return pltpu.make_async_remote_copy(
+            src_ref=src, dst_ref=dst, send_sem=send, recv_sem=recv, device_id=dev, device_id_type=MESH)
+
+    def slab(bb, ss):
+        return land_ref.at[bb, pl.ds(pl.multiple_of(ss * cap, 8), cap)]
+
+    def there(k, j):
+        return ((z + k) % Z) * 2 + j
+
+    def arrived(bb, ss):
+        remote(slab(bb, ss), slab(bb, ss), disp_sem.at[0], recv_sem.at[bb, ss], sib).wait_recv()
+
+    def hand_own(ss):
+        arrived(b, ss)
+        remote(slab(b, ss), slab(b, ss), pass_sem.at[ss, 0], recv_sem.at[b, ss], nx).start()
+        remote(slab(b, ss), slab(b, ss), pass_sem.at[ss, 1], recv_sem.at[b, ss], sib).start()
+
+    def hand_near(ss):
+        arrived(near, ss)
+        remote(slab(near, ss), slab(near, ss), pass_sem.at[ss, 2], recv_sem.at[near, ss], sib).start()
+
+    def load(k, bb):
+        zz = (z + k) % Z
+        return pltpu.make_async_copy(
+            land_ref.at[bb, pl.ds(pl.multiple_of(zz * two, 8), two)],
+            xbuf.at[k, pl.ds(pl.multiple_of(bb * two, 16), two)], load_sem.at[k, bb])
+
+    def dispatch(k, j):
+        to = ((z + Z - k) % Z) * 2 + j
+        return remote(rows_ref.at[to], slab(b, s), disp_sem.at[2 * k + j], recv_sem.at[b, s], (b, to))
+
+    dispatch(0, 1 - y).start()
+    own = [remote(rows_ref.at[s], slab(b, s), pass_sem.at[s, i], recv_sem.at[b, s], dev)
+           for i, dev in enumerate((nx, sib))]
+    for cp in own:
+        cp.start()
+    local = pltpu.make_async_copy(rows_ref.at[s], slab(b, s), local_sem)
+    local.start()
+    for k in range(1, Z):
+        for j in range(2):
+            dispatch(k, j).start()
+
+    hand_own(z * 2 + 1 - y)
+    local.wait()
+    load(0, b).start()
+    for j in range(2):
+        hand_near(z * 2 + j)
+    load(0, near).start()
+    for bb in (beside, across):
+        for j in range(2):
+            arrived(bb, z * 2 + j)
+        load(0, bb).start()
+
+    def compute(k):
+        for n in range(0, width, WIDE):
+            cols = slice(n, n + WIDE)
+            hid[:, cols] = dot(xbuf[k, :, :width], up_ref[:, cols])
+            gact[:, cols] = dot_nt(xbuf[k, :, width:], down_ref[cols, :])
+
+        def sixteen(r, carry):
+            at = pl.ds(pl.multiple_of(r * 16, 16), 16)
+            to = pl.ds(pl.multiple_of(k * block + r * 16, 16), 16)
+            h = hid[at, :]
+            half = 0.5 * (1.0 + erf(h * math.sqrt(0.5)))
+            act[to, :] = (h * half).astype(bf16)
+            slope = half + h * (jnp.exp(-0.5 * h * h) * (1.0 / math.sqrt(2.0 * math.pi)))
+            ghid[to, :] = (gact[at, :] * slope).astype(bf16)
+            return carry
+        lax.fori_loop(0, block // 16, sixteen, 0)
+        mine = pl.ds(pl.multiple_of(k * block, 16), block)
+        for n in range(0, width, WIDE):
+            part[k, :, n : n + WIDE] = dot(act[mine, :], down_ref[:, n : n + WIDE]).astype(bf16)
+            part[k, :, width + n : width + n + WIDE] = dot_nt(ghid[mine, :], up_ref[n : n + WIDE, :]).astype(bf16)
+
+    def share(k, bb):
+        return part.at[k, pl.ds(pl.multiple_of(bb * two, 16), two)]
+
+    def to_sib(k, g):
+        xx = me.x if g else 1 - me.x
+        return remote(share(k, xx * 2 + 1 - me.c), sib_buf.at[k, g], sib_send.at[k, g], sib_recv.at[k, g], sib)
+
+    def to_near(k):
+        return remote(far_sum.at[k], near_buf.at[k], near_send.at[k], near_recv.at[k], nx)
+
+    def join_sib(k):
+        to_sib(k, 0).wait_recv()
+        far_sum[k] = (share(k, near)[...].astype(f32) + sib_buf[k, 0].astype(f32)).astype(bf16)
+        to_near(k).start()
+
+    def to_home(k, j):
+        return remote(own_sum.at[k, j], back_ref.at[s], final_send.at[k, j], final_recv.at[s], (b, there(k, j)))
+
+    def keep_home():
+        return pltpu.make_async_copy(own_sum.at[0, y], back_ref.at[s], final_local)
+
+    def join_near(k):
+        to_sib(k, 1).wait_recv()
+        to_near(k).wait_recv()
+        total = share(k, b)[...].astype(f32) + sib_buf[k, 1].astype(f32) + near_buf[k].astype(f32)
+        for j in range(2):
+            own_sum[k, j] = total[j * cap : (j + 1) * cap].astype(bf16)
+
+        def send():
+            for j in range(2):
+                to_home(k, j).start()
+        if isinstance(k, int) and k > 0:
+            send()
+        else:
+            pl.when(k > 0)(send)
+
+            @pl.when(k == 0)
+            def _():
+                keep_home().start()
+                to_home(0, 1 - y).start()
+
+    def step(k, carry):
+        @pl.when(k < Z - 1)
+        def _():
+            for j in range(2):
+                hand_own(there(k + 1, j))
+        for bb in range(4):
+            load(k, bb).wait()
+        compute(k)
+        for g in range(2):
+            to_sib(k, g).start()
+
+        @pl.when(k < Z - 1)
+        def _():
+            load(k + 1, b).start()
+            for j in range(2):
+                hand_near(there(k + 1, j))
+            load(k + 1, near).start()
+
+        @pl.when(k >= 1)
+        def _():
+            join_sib(k - 1)
+
+        @pl.when(k >= 2)
+        def _():
+            join_near(k - 2)
+
+        @pl.when(k < Z - 1)
+        def _():
+            for bb in (beside, across):
+                for j in range(2):
+                    arrived(bb, there(k + 1, j))
+                load(k + 1, bb).start()
+        return carry
+    lax.fori_loop(0, Z, step, 0)
+
+    everything = (Z * block, width)
+    x, g = xbuf[:, :, :width].reshape(everything), xbuf[:, :, width:].reshape(everything)
+    join_near(Z - 2)
+    for n in range(0, width, WIDE):
+        ddown_ref[n : n + WIDE, :] = dot_tn(act[:, n : n + WIDE], g)
+        if n == 0:
+            join_sib(Z - 1)
+    for n in range(0, width, WIDE):
+        if n == WIDE:
+            join_near(Z - 1)
+        dup_ref[:, n : n + WIDE] = dot_tn(x, ghid[:, n : n + WIDE])
+
+    for k in range(1, seq):
+        e = (s + k) % seq
+        remote(back_ref.at[e], back_ref.at[e], disp_sem.at[0], final_recv.at[e], sib).wait_recv()
+    keep_home().wait()
+    dispatch(0, 1 - y).wait_send()
+    for cp in own:
+        cp.wait_send()
+    for j in range(2):
+        remote(slab(near, z * 2 + j), slab(near, z * 2 + j), pass_sem.at[z * 2 + j, 2], recv_sem.at[b, 0], sib).wait_send()
+    for i in range(2):
+        ss = z * 2 + 1 - y
+        remote(slab(b, ss), slab(b, ss), pass_sem.at[ss, i], recv_sem.at[b, 0], sib).wait_send()
+    to_home(0, 1 - y).wait_send()
+
+    def settle(k, carry):
+        for g in range(2):
+            to_sib(k, g).wait_send()
+        to_near(k).wait_send()
+
+        @pl.when(k > 0)
+        def _():
+            for j in range(2):
+                dispatch(k, j).wait_send()
+                to_home(k, j).wait_send()
+                ss = there(k, j)
+                for i in range(3):
+                    remote(slab(b, ss), slab(b, ss), pass_sem.at[ss, i], recv_sem.at[b, 0], sib).wait_send()
+        return carry
+    lax.fori_loop(0, Z, settle, 0)
+
+
+def moe_rows(batch, seq, sent, up, down):
+    width, hidden_share = up.shape
+    capacity, wide = sent.shape[1:]
+    block = seq * capacity
+    if tuned(batch, seq) and hidden_share == width and capacity % 8 == 0:
+        Z, two = seq // 2, 2 * capacity
+        dma = pltpu.SemaphoreType.DMA
+        out = pl.pallas_call(
+            functools.partial(moe_kernel, seq),
+            out_shape=[
+                like(seq, capacity, wide, dtype=bf16),
+                like(batch, block, wide, dtype=bf16),
+                like(width, hidden_share),
+                like(hidden_share, width),
+            ],
+            in_specs=[HBM, VM, VM],
+            out_specs=[HBM, HBM, VM, VM],
+            scratch_shapes=[
+                pltpu.VMEM((Z, 4 * two, wide), bf16),
+                pltpu.VMEM((Z, 4 * two, wide), bf16),
+                pltpu.VMEM((Z * 4 * two, hidden_share), bf16),
+                pltpu.VMEM((Z * 4 * two, hidden_share), bf16),
+                pltpu.VMEM((4 * two, hidden_share), f32),
+                pltpu.VMEM((4 * two, hidden_share), f32),
+                pltpu.VMEM((Z, 2, two, wide), bf16),
+                pltpu.VMEM((Z, two, wide), bf16),
+                pltpu.VMEM((Z, two, wide), bf16),
+                pltpu.VMEM((Z, 2, capacity, wide), bf16),
+                dma,
+                dma((2 * Z,)),
+                dma((seq, 3)),
+                dma((batch, seq)),
+                dma((Z, batch)),
+                dma((Z, 2)),
+                dma((Z, 2)),
+                dma((Z,)),
+                dma((Z,)),
+                dma((Z, 2)),
+                dma((seq,)),
+                dma,
+            ],
+            compiler_params=pltpu.CompilerParams(
+                collective_id=2, has_side_effects=True, vmem_limit_bytes=56 << 20),
+            name="experts",
+        )(sent, up, down)
+        return out[0], out[2], out[3]
+    mine = lax.all_to_all(sent, "seq", split_axis=0, concat_axis=0, tiled=True)
+    rows = lax.all_gather(mine, "batch", axis=0).reshape(batch * block, wide)
+    part, d_up, d_down = pl.pallas_call(
+        expert_kernel,
+        out_shape=[
+            like(batch * block, wide, dtype=bf16),
+            like(width, hidden_share),
+            like(hidden_share, width),
+        ],
+        grid=(batch,),
+        in_specs=[
+            pl.BlockSpec((block, wide), lambda i: (i, 0)),
+            pl.BlockSpec((width, hidden_share), lambda i: (0, 0)),
+            pl.BlockSpec((hidden_share, width), lambda i: (0, 0)),
+        ],
+        out_specs=[
+            pl.BlockSpec((block, wide), lambda i: (i, 0)),
+            pl.BlockSpec((width, hidden_share), lambda i: (0, 0)),
+            pl.BlockSpec((hidden_share, width), lambda i: (0, 0)),
+        ],
+        compiler_params=params(),
+        name="experts",
+    )(rows, up, down)
+    part = part.reshape((batch,) + sent.shape)
+    mine = lax.psum_scatter(part, "batch", scatter_dimension=0, tiled=False)
+    return lax.all_to_all(mine, "seq", split_axis=0, concat_axis=0, tiled=True), d_up, d_down
+
+
 def body(
     tokens,
     in_proj,
@@ -1095,8 +1327,7 @@
         compiler_params=params(),
         name="enter",
     )(tok, halo, in_full, small, vec, gain)
-    rates = -jnp.exp(vec[:states])
-    before = chain_states(seq, True, dsum, rates, end)
+    before = relay_states(batch, seq, True, states, dsum, vec, end)
     size = GROUP * states
     total = experts * capacity
     hist, y, hid, gated, moe_in, gate, sent = pl.pallas_call(
@@ -1122,31 +1353,9 @@
         name="leave",
     )(tok, cot, before, dt, u, z, proj, vec, out_full, gain, router, route, slot, place.reshape(1, count))
 
-    spread = spread_rows(batch, seq, sent.reshape(experts, capacity, 2 * width))
-    block = seq * capacity
-    hidden_share = expert_up.shape[2]
-    part, d_up, d_down = pl.pallas_call(
-        expert_kernel,
-        out_shape=[
-            like(batch * block, 2 * width, dtype=bf16),
-            like(width, hidden_share),
-            like(hidden_share, width),
-        ],
-        grid=(batch,),
-        in_specs=[
-            pl.BlockSpec((block, 2 * width), lambda i: (i, 0)),
-            pl.BlockSpec((width, hidden_share), lambda i: (0, 0)),
-            pl.BlockSpec((hidden_share, width), lambda i: (0, 0)),
-        ],
-        out_specs=[
-            pl.BlockSpec((block, 2 * width), lambda i: (i, 0)),
-            pl.BlockSpec((width, hidden_share), lambda i: (0, 0)),
-            pl.BlockSpec((hidden_share, width), lambda i: (0, 0)),
-        ],
-        compiler_params=params(),
-        name="experts",
-    )(spread.reshape(batch * block, 2 * width), expert_up[0], expert_down[0])
-    back = collect_rows(batch, seq, part.reshape(batch, seq, capacity, 2 * width)).reshape(total, 2 * width)
+    back, d_up, d_down = moe_rows(
+        batch, seq, sent.reshape(experts, capacity, 2 * width), expert_up[0], expert_down[0])
+    back = back.reshape(total, 2 * width)
 
     block_out, ghid, gy, gz, d_out, d_router, d_skip, d_moe, adj = pl.pallas_call(
         partial(return_kernel, dims),
@@ -1166,7 +1375,7 @@
         compiler_params=params(),
         name="back_experts",
     )(back, cot, hid, moe_in, gate, gated, y, u, z, dt, proj, vec, out_full, gain, router, route, place)
-    later = chain_states(seq, False, dsum, rates, adj)
+    later = relay_states(batch, seq, False, states, dsum, vec, adj)
     d_tok, d_halo, d_in, d_small, d_vec, d_norm = pl.pallas_call(
         partial(back_kernel, dims),
         out_shape=[
@@ -1181,8 +1390,9 @@
         out_specs=[VM] * 6,
         scratch_shapes=[
             pltpu.VMEM((2, size + states, inner), bf16),
-            pltpu.VMEM((size, WIDE), bf16),
-            pltpu.VMEM((size, WIDE), bf16),
+            pltpu.VMEM((GROUP, states, tile), f32),
+            pltpu.VMEM((GROUP, states, tile), f32),
+            pltpu.VMEM((GROUP, states, tile), f32),
             pltpu.VMEM((GROUP, states, tile), f32),
             pltpu.VMEM((states, inner), f32),
             pltpu.VMEM((count, inner), f32),

time: 408 us -> 374 us (0.917); the launches traced: 406 us -> 367 us
  Pallas kernels: 361 us -> 318 us
  local copies, waits for them, and re-layouts: 29.6 us -> 33.9 us
    pallas_call x5 -> x3, Pallas kernels: 146 us -> 114 us  [the longest x1 85.3 us: moe_rows(): pl.pallas_call(functools.partial(moe_kernel, seq), out_shape=[like(seq, c...]
    pallas_call x1, Pallas kernels: 56 us -> 41.5 us  [body(): pl.pallas_call(partial(back_kernel, dims), out_shape=[like(count, width),...]
    unnamed x40 -> x38, local copies, waits for them, and re-layouts: 13.6 us -> 15.3 us
  transfers between devices with their start and end apart: 2 -> 2, of which waited for: 1 -> 0; matrix products, arithmetic and copies ran while one was open for 5% -> 6% of each run, Pallas kernels for 10% -> 11%
where the time goes in v2:
time: 374 us; the launch traced here: 367 us
  Pallas kernels  318 us (85%)
  local copies, waits for them, and re-layouts  33.9 us (9%)
  other arithmetic  7.16 us (2%)
  starting transfers between devices  6.16 us (2%)
    pallas_call x1, Pallas kernels, moe_rows(): pl.pallas_call(functools.partial(moe_kernel, seq), out_shape=[like(seq, c...  85.3 us
    pallas_call x1, Pallas kernels, reduce_all(): pl.pallas_call(functools.partial(reduce_kernel, batch, seq, n), out_shape...  70.6 us
    pallas_call x1, Pallas kernels, body(): pl.pallas_call(partial(back_kernel, dims), out_shape=[like(count, width),...  41.5 us
    pallas_call x1, Pallas kernels, gather_all(): pl.pallas_call(functools.partial(gather_kernel, batch, seq, n), out_shape...  40.7 us
    pallas_call x2, Pallas kernels, relay_states(): pl.pallas_call(functools.partial(relay_kernel, seq, forward, states), out...  28.7 us
    pallas_call x1, Pallas kernels, body(): pl.pallas_call(partial(leave_kernel, dims, capacity), out_shape=[like(seq...  19.5 us
    pallas_call x1, Pallas kernels, body(): pl.pallas_call(partial(return_kernel, dims), out_shape=[like(count, width...  16.6 us
    pallas_call x1, Pallas kernels, body(): pl.pallas_call(partial(enter_kernel, dims), out_shape=[like(seqs, rows +...  15.6 us
  transfers between devices with their start and end apart: 2, of which 0 were waited for; matrix products, arithmetic and copies ran while one was open for 6% of the time, Pallas kernels for 11%

profile of v2, /device:TPU:0, one launch (start us, length us, event | category | flops | bytes accessed | tf_op | source)
XLA Modules:
  0.0 367.1 jit_solution(3490811968429145612)
XLA Ops:
  0.7 0.8 slice.104
  1.4 4.9 %collective-permute-start = (bf16[2,3,768]{2,1,0:T(4,128)(2,1)S(1)}, bf16[2,3,768]{2,1,0:T(4,128)(2,1)S(1)}, u32[]{:S(2)}, u32[]{:S(2)}) collective-permute-start(bf16[2,3,768]{2,1,0:T(4,128)(2,1)S(1)} %slice.104), channel_id=1, source_target_pairs={{0,1},{1,2},{2,3},{3,4},{4,5},{5,6},{6,7},{8,9},{9,10},{10,11},{11... | collective-permute-start | bytes 27656 | tf_op jit(solution)/shard_map/ppermute | solution.py:1295
  6.3 0.7 copy.116
  7.8 0.8 copy.115
  8.6 0.8 copy.111
  9.3 0.8 copy.112
  10.1 0.8 copy.109
  10.9 0.8 copy.113
  11.7 0.8 copy.110
  12.4 0.8 copy.114
  13.4 1.4 pad_maximum_fusion.2.refs_2_
  14.8 40.7 %gather_weights.1 = (bf16[768,3072]{1,0:T(8,128)(2,1)}, bf16[1536,768]{1,0:T(8,128)(2,1)}, bf16[1536,256]{1,0:T(8,128)(2,1)}) custom-call(bf16[24,3072]{1,0:T(8,128)(2,1)} %refs_0_.1, bf16[48,768]{1,0:T(8,128)(2,1)} %refs_1_.1, bf16[48,256]{1,0:T(8,128)(2,1)} %pad_maximum_fusion.2.refs_2_), custom_call_target="tpu_custom_call" | custom-call | tf_op jit(solution)/shard_map/gather_weights/pallas_call | solution.py:172
  55.5 1.2 slice.107
  56.7 1.5 copy.118
  60.5 0.8 slice.105.small_ref
  63.4 15.6 %enter.1 = (f32[2,136,1536]{2,1,0:T(8,128)}, f32[256,1536]{1,0:T(8,128)}, f32[256,1536]{1,0:T(8,128)}, f32[256,1536]{1,0:T(8,128)}, f32[256,128]{1,0:T(8,128)}, ...) custom-call(bf16[256,768]{1,0:T(8,128)(2,1)} %bitcast.40, bf16[16,768]{1,0:T(8,128)(2,1)} %pad_bitcast_fusion.halo_ref, ...), custom_call_target="tpu_custom_call" | custom-call | tf_op jit(solution)/shard_map/enter/pallas_call | solution.py:1313
  79.0 9.1 %relay_forward.1.h0_ref = f32[2,16,1536]{2,1,0:T(8,128)} custom-call(f32[2,1,1536]{2,1,0:T(1,128)} %get-tuple-element.80.dsum_ref, f32[24,1536]{1,0:T(8,128)} %convert_bitcast_fusion.1.vec_ref, f32[2,16,1536]{2,1,0:T(8,128)} %get-tuple-element.81.end_ref), custom_call_target="tpu_custom_call" | custom-call | tf_op jit(solution)/shard_map/relay_forward/pallas_call | solution.py:499
  88.0 19.5 %leave.1 = (bf16[2,2064,1536]{2,1,0:T(8,128)(2,1)}, f32[256,1536]{1,0:T(8,128)}, f32[256,768]{1,0:T(8,128)}, bf16[256,1536]{1,0:T(8,128)(2,1)}, bf16[256,768]{1,...) custom-call(bf16[256,768]{1,0:T(8,128)(2,1)} %bitcast.41, bf16[256,768]{1,0:T(8,128)(2,1)} %bitcast.47, ...), custom_call_target="tpu_custom_call" | custom-call | tf_op jit(solution)/shard_map/leave/pallas_call | solution.py:1333
  107.6 85.3 %experts.1 = (bf16[8,40,1536]{2,1,0:T(8,128)(2,1)}, bf16[4,320,1536]{2,1,0:T(8,128)(2,1)}, f32[768,768]{1,0:T(8,128)}, f32[768,768]{1,0:T(8,128)}) custom-call(bf16[8,40,1536]{2,1,0:T(8,128)(2,1)} %bitcast.54, bf16[768,768]{1,0:T(8,128)(2,1)} %bitcast.51, bf16[768,768]{1,0:T(8,128)(2,1)} %bitcast.52), custom_call_target="tpu_custom_call" | custom-call | tf_op jit(solution)/shard_map/experts/pallas_call | solution.py:1181
  192.8 16.6 %back_experts.1 = (bf16[256,768]{1,0:T(8,128)(2,1)}, f32[256,768]{1,0:T(8,128)}, f32[256,1536]{1,0:T(8,128)}, bf16[256,1536]{1,0:T(8,128)(2,1)}, bf16[1536,768]{...) custom-call(bf16[320,1536]{1,0:T(8,128)(2,1)} %bitcast.53, ...), custom_call_target="tpu_custom_call" | custom-call | tf_op jit(solution)/shard_map/back_experts/pallas_call | solution.py:1360
  210.4 19.6 %relay_backward.1.later_ref = f32[2,16,1536]{2,1,0:T(8,128)} custom-call(f32[2,1,1536]{2,1,0:T(1,128)} %get-tuple-element.80.dsum_ref, f32[24,1536]{1,0:T(8,128)} %convert_bitcast_fusion.1.vec_ref, f32[2,16,1536]{2,1,0:T(8,128)} %get-tuple-element.97.end_ref), custom_call_target="tpu_custom_call" | custom-call | tf_op jit(solution)/shard_map/relay_backward/pallas_call | solution.py:499
  230.0 41.5 %back_mixer.1 = (f32[256,768]{1,0:T(8,128)}, f32[16,768]{1,0:T(8,128)}, bf16[768,3072]{1,0:T(8,128)(2,1)}, bf16[1536,128]{1,0:T(8,128)(2,1)}, f32[24,1536]{1,0:T(8,128)}, /*index=5*/f32[1,768]{1,0:T(1,128)}) custom-call(bf16[256,768]{1,0:T(8,128)(2,1)} %bitcast.42, bf16[16,768]{1,0:T(8,128)(2,1)} %pad_bitcast_fusion.halo_ref, ...), custom_call_target="tpu_custom_call" | custom-call | tf_op jit(solution)/shard_map/back_mixer/pallas_call | solution.py:1379
  273.0 0.9 copy.129
  274.2 3.4 scatter.4
  277.6 1.4 pad_maximum_fusion.refs_2_
  279.0 2.3 copy-done
  281.3 70.6 %reduce_grads.1 = (f32[24,3072]{1,0:T(8,128)S(1)}, f32[48,768]{1,0:T(8,128)S(1)}, f32[48,256]{1,0:T(8,128)S(1)}) custom-call(bf16[768,3072]{1,0:T(8,128)(2,1)S(1)} %copy-done, bf16[1536,768]{1,0:T(8,128)(2,1)S(1)} %copy-done.1, bf16[1536,256]{1,0:T(8,128)(2,1)S(1)} %pad_maximum_fusion.refs_2_), custom_call_target="tpu_custom_call" | custom-call | tf_op jit(solution)/shard_map/reduce_grads/pallas_call | solution.py:348
  352.1 1.3 collective-permute-start.1
  358.2 0.8 slice_add_fusion
  359.0 1.5 scatter-add.4
  361.9 3.4 copy.154
  365.2 1.4 copy.155
  (65 shorter events, 14.3 us)
Async XLA Ops:
  0.6 57.5 %copy-start.10 = (s32[2,128]{1,0:T(2,128)S(1)}, s32[2,128]{1,0:T(2,128)}, u32[]{:S(2)}) copy-start(s32[2,128]{1,0:T(2,128)} %param.37) | copy-start | bytes 3076
  0.7 57.6 %copy-start.11 = (s32[2,128]{1,0:T(2,128)S(1)}, s32[2,128]{1,0:T(2,128)}, u32[]{:S(2)}) copy-start(s32[2,128]{1,0:T(2,128)} %param.38) | copy-start | bytes 3076
  1.4 61.4 %collective-permute-start = (bf16[2,3,768]{2,1,0:T(4,128)(2,1)S(1)}, bf16[2,3,768]{2,1,0:T(4,128)(2,1)S(1)}, u32[]{:S(2)}, u32[]{:S(2)}) collective-permute-start(bf16[2,3,768]{2,1,0:T(4,128)(2,1)S(1)} %slice.104), channel_id=1, source_target_pairs={{0,1},{1,2},{2,3},{3,4},{4,5},{5,6},{6,7},{8,9},{9,10},{10,11},{11... | collective-permute-start | bytes 27656 | tf_op jit(solution)/shard_map/ppermute | solution.py:1295
  56.6 3.9 %copy-start.2 = (bf16[1536,256]{1,0:T(8,128)(2,1)S(1)}, bf16[1536,256]{1,0:T(8,128)(2,1)}, u32[]{:S(2)}) copy-start(bf16[1536,256]{1,0:T(8,128)(2,1)} %get-tuple-element.79) | copy-start | bytes 2359300
  58.3 4.5 %copy-start.4 = (s32[256,1]{1,0:T(8,128)}, s32[256,1]{1,0:T(8,128)S(1)}, u32[]{:S(2)}) copy-start(s32[256,1]{1,0:T(8,128)S(1)} %copy.121.route_ref) | copy-start | bytes 3076
  58.4 4.3 %copy-start.5 = (s32[256,1]{1,0:T(8,128)}, s32[256,1]{1,0:T(8,128)S(1)}, u32[]{:S(2)}) copy-start(s32[256,1]{1,0:T(8,128)S(1)} %copy.122.slot_ref) | copy-start | bytes 3076
  229.9 42.5 %copy-start.7 = (f32[768,128]{1,0:T(8,128)S(1)}, f32[768,128]{1,0:T(8,128)}, u32[]{:S(2)}) copy-start(f32[768,128]{1,0:T(8,128)} %get-tuple-element.108) | copy-start | bytes 1179652
  271.5 1.5 copy-start.6
  271.5 2.5 copy-start.9
  274.0 5.0 %copy-start.1 = (bf16[1536,768]{1,0:T(8,128)(2,1)S(1)}, bf16[1536,768]{1,0:T(8,128)(2,1)}, u32[]{:S(2)}) copy-start(bf16[1536,768]{1,0:T(8,128)(2,1)} %get-tuple-element.104.refs_1_) | copy-start | bytes 7077892
  279.0 2.3 copy-start
  281.3 70.7 %copy-start.8 = (f32[16,768]{1,0:T(8,128)S(1)}, f32[16,768]{1,0:T(8,128)}, u32[]{:S(2)}) copy-start(f32[16,768]{1,0:T(8,128)} %get-tuple-element.102) | copy-start | bytes 147460
  352.1 6.2 %collective-permute-start.1 = (f32[2,3,768]{2,1,0:T(4,128)S(1)}, f32[2,3,768]{2,1,0:T(4,128)S(1)}, u32[]{:S(2)}, u32[]{:S(2)}) collective-permute-start(f32[2,3,768]{2,1,0:T(4,128)S(1)} %slice.130), channel_id=1, source_target_pairs={{1,0},{2,1},{3,2},{4,3},{5,4},{6,5},{7,6},{9,8},{10,9},{11,10},{12... | collective-permute-start | bytes 55304 | tf_op jit(solution)/shard_map/ppermute | solution.py:1425
  361.9 3.4 copy-start.3
